TPU v7x, 32 devices: a whole 2x2x4 slice. The times are simulated.
32 devices in a mesh: ctx: 8 (over z, x), tp: 4 (over y, core).
Axes of the slice: x: 2, y: 2, z: 4, core: 2. Of those that a mesh axis runs over, the one named last changes fastest.
Arguments:
- queries: bfloat16 [8192, 1024], P('tp', 'ctx'), may hold values from -6 to 6
- key_signal: bfloat16 [8192, 1024], P('tp', 'ctx'), may hold values from -6 to 6
- value_signal: bfloat16 [8192, 1024], P('tp', 'ctx'), may hold values from -6 to 6
- cotangent: bfloat16 [8192, 1024], P('tp', 'ctx'), may hold values from -6 to 6
- short_weight: float32 [3, 7, 8192], P(None, None, 'tp'), may hold values from -2 to 2
- residues: float32 [8192, 16], P('tp'), may hold values from -1.5 to 1.5
- decay_rates: float32 [8192, 16], P('tp'), may hold values from 0.0001 to 0.03
- skip_gain: float32 [8192], P('tp'), may hold values from 0.5 to 1.5
Outputs:
- mixed: bfloat16 [8192, 1024], P('tp', 'ctx')
- grad_queries: bfloat16 [8192, 1024], P('tp', 'ctx')
- grad_keys: bfloat16 [8192, 1024], P('tp', 'ctx')
- grad_values: bfloat16 [8192, 1024], P('tp', 'ctx')
- grad_short: float32 [3, 7, 8192], P(None, None, 'tp')
- grad_residues: float32 [8192, 16], P('tp')
- grad_skip: float32 [8192], P('tp')
All inputs are finite; a program needn't handle non-finite values.
Results may differ from a plain program's by a relative error of at most 0.015.
Values may be sent and summed in bfloat16 or wider, within the bound.
A program may use at most 128 MiB of HBM per device.

v0:
```python
import functools
import math

import jax
import jax.numpy as jnp
import ml_dtypes
import numpy as np
from jax import lax
from jax.experimental import pallas as pl
from jax.experimental.pallas import tpu as pltpu
from jax.sharding import PartitionSpec as P

F32 = jnp.float32
BF16 = jnp.bfloat16
NODES = 16


def two(table):
    high = table.astype(ml_dtypes.bfloat16)
    low = (table - high.astype(np.float64)).astype(ml_dtypes.bfloat16)
    return high, low


@functools.lru_cache(None)
def tables(rows, modes):
    top = rows - 1
    half = [round(top / 2 - top / 2 * math.cos((2 * k + 1) * math.pi / (2 * NODES))) for k in range(NODES // 2)]
    nodes = np.array(half + [top - x for x in half[::-1]], np.float64)
    basis = np.ones((NODES, rows))
    spots = np.arange(rows, dtype=np.float64)
    for k in range(NODES):
        for other in range(NODES):
            if other != k:
                basis[k] *= (spots - nodes[other]) / (nodes[k] - nodes[other])
    spread = np.tile(basis, (modes, 1))
    back = spread[:, ::-1]
    omega = 2 * math.pi * (np.arange(rows) + 0.5) / (2 * rows)
    angle = spots[:, None] * omega[None, :]
    dft = np.concatenate([np.cos(angle), -np.sin(angle)], 1)
    inv = np.concatenate([np.cos(angle), -np.sin(angle)], 1).T / rows
    out = {}
    out["dft"] = np.concatenate(two(dft), 0)
    out["inv"] = np.concatenate(two(inv), 1)
    out["spec_hi"], out["spec_lo"] = two(spread @ dft)
    out["mom"] = np.concatenate(two(spread.T), 0)
    out["mom_back"] = np.concatenate(two(back.T), 0)
    out["lag_hi"], out["lag_lo"] = two(inv @ spread.T)
    out["out"] = np.concatenate(two(spread), 1)
    out["out_back"] = np.concatenate(two(back), 1)
    eye = np.eye(modes)
    out["times"] = np.kron(eye, nodes[None, :]).astype(ml_dtypes.bfloat16)
    pick = np.kron(eye, np.ones((1, NODES)))
    out["pick"] = pick.astype(ml_dtypes.bfloat16)
    return out


def mm(a, b):
    return lax.dot_general(a, b, (((1,), (0,)), ((), ())), preferred_element_type=F32)


def mm_nt(a, b):
    return lax.dot_general(a, b, (((1,), (1,)), ((), ())), preferred_element_type=F32)


def mm_tn(a, b):
    return lax.dot_general(a, b, (((0,), (0,)), ((), ())), preferred_element_type=F32)


def parts(x, count):
    out = []
    for _ in range(count):
        piece = x.astype(BF16)
        out.append(piece)
        x = x - piece.astype(F32)
    return out


def exact(op, x, table, count):
    total = None
    for piece in parts(x, count):
        term = op(piece, table)
        total = term if total is None else total + term
    return total


def powers_kernel(dec_ref, res_ref, times_ref, pick_ref, hi_ref, lo_ref, pow_ref, spec_ref):
    dec = dec_ref[...]
    gain = res_ref[...] * jnp.sqrt(2.0 * dec)
    powers = jnp.exp(-exact(mm, dec, times_ref[...], 3))
    pow_ref[...] = powers
    high, low = parts(powers * exact(mm, gain, pick_ref[...], 3), 2)
    spec_ref[...] = mm(high, hi_ref[...]) + mm(low, hi_ref[...]) + mm(high, lo_ref[...])


def shifted(x, halo, lane, j):
    rows = x.shape[1]
    if j == 0:
        return x
    return pltpu.roll(jnp.where(lane >= rows - j, halo, x), j, 1)


def near_kernel(taps, q_ref, k_ref, v_ref, cot_ref, halo_ref, w_ref, pow_ref, spec_ref,
                place_ref, dft_ref, inv_ref, mom_ref, back_ref, laghi_ref, laglo_ref, pick_ref,
                qs_ref, ks_ref, vs_ref, near_ref, grad_ref, state_ref, res_ref):
    rows = q_ref.shape[1]
    lane = lax.broadcasted_iota(jnp.int32, q_ref.shape, 1)
    halos = mm_tn(halo_ref[...], place_ref[...])
    w = w_ref[...]
    short = []
    for i, ref in enumerate((q_ref, k_ref, v_ref)):
        x = ref[...].astype(F32)
        halo = halos[:, i * rows : (i + 1) * rows]
        total = jnp.zeros(x.shape, F32)
        for j in range(taps):
            at = i * taps + j
            total = total + w[:, at : at + 1] * shifted(x, halo, lane, j)
        short.append(total.astype(BF16))
    qs_ref[...], ks_ref[...], vs_ref[...] = short
    gated = (short[1].astype(F32) * short[2].astype(F32)).astype(BF16)
    gmix = (cot_ref[...].astype(F32) * short[0].astype(F32)).astype(BF16)
    gated2 = jnp.concatenate([gated, gated], 1)
    gmix2 = jnp.concatenate([gmix, gmix], 1)
    z = mm(gated2, dft_ref[...])
    g = mm(gmix2, dft_ref[...])
    h = spec_ref[...]
    zr, zi = z[:, :rows], z[:, rows:]
    gr, gi = g[:, :rows], g[:, rows:]
    hr, hi = h[:, :rows], h[:, rows:]
    fwd = jnp.concatenate([zr * hr - zi * hi, zr * hi + zi * hr], 1).astype(BF16)
    bwd = jnp.concatenate([gr * hr + gi * hi, gi * hr - gr * hi], 1).astype(BF16)
    lag = jnp.concatenate([gr * zr + gi * zi, gi * zr - gr * zi], 1)
    near = mm(fwd, inv_ref[...])
    near_ref[...] = near[:, :rows] + near[:, rows:]
    grad = mm(bwd, inv_ref[...])
    grad_ref[...] = grad[:, :rows] + grad[:, rows:]
    powers = pow_ref[...]
    pick = pick_ref[...]
    state = powers * mm(gated2, back_ref[...])
    modes = pick.shape[0]

    def folded(x):
        high, low = parts(x, 2)
        return mm_nt(pick, high) + mm_nt(pick, low)

    state_ref[:modes, :] = folded(state)
    state_ref[modes:, :] = folded(powers * mm(gmix2, mom_ref[...]))
    high, low = parts(lag, 2)
    moments = mm(high, laghi_ref[...]) + mm(low, laghi_ref[...]) + mm(high, laglo_ref[...])
    res_ref[...] = folded(powers * moments)


def far_kernel(taps, me_ref, q_ref, k_ref, v_ref, cot_ref, halo_ref, qs_ref, ks_ref, vs_ref,
               near_ref, grad_ref, pow_ref, all_ref, state_ref, res_ref, dec_ref, amp_ref, skip_ref,
               place_ref, out_ref, back_ref, pick_ref, sums_ref,
               mixed_ref, gq_ref, gk_ref, gv_ref, head_ref, part_ref):
    rows = q_ref.shape[1]
    lane = lax.broadcasted_iota(jnp.int32, q_ref.shape, 1)
    me = me_ref[0]
    count = all_ref.shape[0]
    modes = dec_ref.shape[0]
    dec = dec_ref[...]
    root = jnp.sqrt(2.0 * dec)
    one = jnp.exp(-dec)
    chunk = jnp.exp(-dec * float(rows))
    zero = jnp.zeros(dec.shape, F32)

    def ahead(p, s):
        return jnp.where(p < me, s * chunk + all_ref[p, :modes, :].astype(F32), s)

    def behind(i, r):
        p = count - 1 - i
        return jnp.where(p > me, r * chunk + all_ref[p, modes:, :].astype(F32), r)

    s_in = lax.fori_loop(0, count, ahead, zero, unroll=8)
    r_in = lax.fori_loop(0, count, behind, zero, unroll=8)
    part_ref[:modes, :] = root * (res_ref[...] + one * s_in * state_ref[modes:, :])
    gain = amp_ref[...] * root * one
    powers = pow_ref[...]
    pick = pick_ref[...]

    def spread(x, table_ref):
        high, low = parts(powers * exact(mm_tn, x, pick, 2), 2)
        full = mm(high, table_ref[...]) + mm(low, table_ref[...])
        return full[:, :rows] + full[:, rows:]

    conv = (near_ref[...] + spread(gain * s_in, out_ref)).astype(BF16)
    gconv = (grad_ref[...] + spread(gain * r_in, back_ref)).astype(BF16)
    skip = skip_ref[...]
    qs, ks, vs = qs_ref[...].astype(F32), ks_ref[...].astype(F32), vs_ref[...].astype(F32)
    cot = cot_ref[...].astype(F32)
    gated = (ks * vs).astype(BF16).astype(F32)
    gmix = (cot * qs).astype(BF16).astype(F32)
    mix = conv.astype(F32) + skip * gated
    mixed_ref[...] = (qs * mix).astype(BF16)
    gq = (cot * mix).astype(BF16)
    ggated = gconv.astype(F32) + skip * gmix
    gk = (ggated * vs).astype(BF16)
    gv = (ggated * ks).astype(BF16)
    gq_ref[...], gk_ref[...], gv_ref[...] = gq, gk, gv
    first = (lax.broadcasted_iota(jnp.int32, (8, rows), 0) == lax.broadcasted_iota(jnp.int32, (8, rows), 1)).astype(BF16)
    head_ref[...] = jnp.concatenate([mm_nt(first, x) for x in (gq, gk, gv)], 0).astype(BF16)
    halos = mm_tn(halo_ref[...], place_ref[...])
    products = []
    for i, (ref, grads) in enumerate(((q_ref, gq), (k_ref, gk), (v_ref, gv))):
        x = ref[...].astype(F32)
        values = grads.astype(F32)
        halo = halos[:, i * rows : (i + 1) * rows]
        for j in range(taps):
            products.append((values * shifted(x, halo, lane, j)).astype(BF16))
    products.append((gmix * gated).astype(BF16))
    sums = mm(jnp.concatenate(products, 1), sums_ref[...])
    part_ref[modes:, :] = sums.T[:24, :]


def last_kernel(taps, gq_ref, gk_ref, gv_ref, halo_ref, w_ref, place_ref, oq_ref, ok_ref, ov_ref):
    rows = gq_ref.shape[1]
    lane = lax.broadcasted_iota(jnp.int32, gq_ref.shape, 1)
    halos = mm_tn(halo_ref[...], place_ref[...])
    w = w_ref[...]
    for i, (ref, out) in enumerate(((gq_ref, oq_ref), (gk_ref, ok_ref), (gv_ref, ov_ref))):
        x = ref[...].astype(F32)
        halo = halos[:, i * rows : (i + 1) * rows]
        total = jnp.zeros(x.shape, F32)
        for j in range(taps):
            moved = x if j == 0 else pltpu.roll(jnp.where(lane < j, halo, x), rows - j, 1)
            at = i * taps + j
            total = total + w[:, at : at + 1] * moved
        out[...] = total.astype(BF16)


def passed_along(block, axis, distance):
    devices = range(lax.axis_size(axis))
    route = [(i - distance, i) for i in devices if i - distance in devices]
    return lax.ppermute(block, axis, route)


def per_device(
    queries, key_signal, value_signal, cotangent, short_weight, residues, decay_rates, skip_gain
):
    channels, rows = queries.shape
    taps = short_weight.shape[1]
    modes = residues.shape[1]
    devices = lax.axis_size("ctx")
    block = min(256, channels)
    grid = (channels // block,)
    tab = {name: jnp.asarray(value) for name, value in tables(rows, modes).items()}
    wide = modes * NODES
    tail = np.zeros((24, 3 * rows), np.float32)
    head = np.zeros((24, 3 * rows), np.float32)
    for i in range(3):
        for j in range(8):
            tail[i * 8 + j, i * rows + rows - 8 + j] = 1
            head[i * 8 + j, i * rows + j] = 1
    tail, head = jnp.asarray(tail, BF16), jnp.asarray(head, BF16)
    sums = np.zeros(((3 * taps + 1) * rows, 128), np.float32)
    for i in range(3 * taps + 1):
        sums[i * rows : (i + 1) * rows, i] = 1
    sums = jnp.asarray(sums, BF16)

    def tall(width):
        return pl.BlockSpec((block, width), lambda i: (i, 0))

    def flat(height):
        return pl.BlockSpec((height, block), lambda i: (0, i))

    def whole(x):
        return pl.BlockSpec(x.shape, lambda i: (0,) * x.ndim)

    def shape(*dims, kind=F32):
        return jax.ShapeDtypeStruct(dims, kind)

    params = pltpu.CompilerParams(vmem_limit_bytes=48 * 1024 * 1024)
    sent = jnp.concatenate([x[:, rows - 8 :].T for x in (queries, key_signal, value_signal)], 0)
    left = passed_along(sent, "ctx", 1)
    w_tall = short_weight.reshape(3 * taps, channels).T
    dec_flat = decay_rates.T
    amp_flat = residues.T
    skip = skip_gain[:, None]

    args = (tab["times"], tab["pick"], tab["spec_hi"], tab["spec_lo"])
    powers, spec = pl.pallas_call(
        powers_kernel,
        grid=grid,
        in_specs=[tall(modes), tall(modes)] + [whole(x) for x in args],
        out_specs=[tall(wide), tall(2 * rows)],
        out_shape=[shape(channels, wide), shape(channels, 2 * rows)],
        compiler_params=params,
        cost_estimate=pl.CostEstimate(flops=10**9, bytes_accessed=5 * 10**6, transcendentals=10**6),
        name="powers",
    )(decay_rates, residues, *args)

    args = (tail, tab["dft"], tab["inv"], tab["mom"], tab["mom_back"], tab["lag_hi"], tab["lag_lo"], tab["pick"])
    q_short, k_short, v_short, near, grad, state, res = pl.pallas_call(
        functools.partial(near_kernel, taps),
        grid=grid,
        in_specs=[tall(rows)] * 4 + [flat(24), tall(3 * taps), tall(wide), tall(2 * rows)] + [whole(x) for x in args],
        out_specs=[tall(rows)] * 5 + [flat(2 * modes), flat(modes)],
        out_shape=[shape(channels, rows, kind=BF16)] * 3 + [shape(channels, rows)] * 2 + [shape(2 * modes, channels), shape(modes, channels)],
        compiler_params=params,
        name="near",
    )(queries, key_signal, value_signal, cotangent, left, w_tall, powers, spec, *args)

    every = lax.all_gather(state.astype(BF16), "ctx")
    me = lax.axis_index("ctx").astype(jnp.int32).reshape(1)
    args = (tail, tab["out"], tab["out_back"], tab["pick"], sums)
    mixed, gq, gk, gv, heads, part = pl.pallas_call(
        functools.partial(far_kernel, taps),
        grid=grid,
        in_specs=[pl.BlockSpec(memory_space=pltpu.SMEM)] + [tall(rows)] * 4 + [flat(24)] + [tall(rows)] * 5
        + [tall(wide), pl.BlockSpec((devices, 2 * modes, block), lambda i: (0, 0, i)), flat(2 * modes), flat(modes), flat(modes), flat(modes), tall(1)]
        + [whole(x) for x in args],
        out_specs=[tall(rows)] * 4 + [flat(24), flat(modes + 24)],
        out_shape=[shape(channels, rows, kind=BF16)] * 4 + [shape(24, channels, kind=BF16), shape(modes + 24, channels)],
        compiler_params=params,
        name="far",
    )(me, queries, key_signal, value_signal, cotangent, left, q_short, k_short, v_short, near, grad,
      powers, every, state, res, dec_flat, amp_flat, skip, *args)

    right = passed_along(heads, "ctx", -1)
    totals = lax.psum(part, "ctx") * (1.0 / math.sqrt(rows * devices))
    grads = pl.pallas_call(
        functools.partial(last_kernel, taps),
        grid=grid,
        in_specs=[tall(rows)] * 3 + [flat(24), tall(3 * taps), whole(head)],
        out_specs=[tall(rows)] * 3,
        out_shape=[shape(channels, rows, kind=BF16)] * 3,
        compiler_params=params,
        cost_estimate=pl.CostEstimate(flops=10**9, bytes_accessed=5 * 10**6, transcendentals=0),
        name="last",
    )(gq, gk, gv, right, w_tall, head)
    return (
        mixed,
        *grads,
        totals[modes : modes + 3 * taps].reshape(3, taps, channels),
        totals[:modes].T,
        totals[modes + 3 * taps],
    )


def solution(mesh):
    signal = P("tp", "ctx")
    in_specs = (signal,) * 4 + (P(None, None, "tp"), P("tp", None), P("tp", None), P("tp"))
    out_specs = (signal,) * 4 + (P(None, None, "tp"), P("tp", None), P("tp"))
    return jax.shard_map(
        per_device, mesh=mesh, in_specs=in_specs, out_specs=out_specs, check_vma=False
    )
```

profile of v0, /device:TPU:0, one launch (start us, length us, event | category | flops | bytes accessed | tf_op | source)
XLA Modules:
  0.0 205.9 jit_solution(5040696662490054854)
XLA Ops:
  7.2 1.3 slice.18
  8.7 1.3 slice.19
  11.2 4.8 %collective-permute-start = (bf16[24,2048]{1,0:T(8,128)(2,1)}, bf16[24,2048]{1,0:T(8,128)(2,1)S(1)}, u32[]{:S(2)}, u32[]{:S(2)}) collective-permute-start(bf16[24,2048]{1,0:T(8,128)(2,1)} %pad_maximum_fusion), channel_id=1, source_target_pairs={{0,4},{4,8},{8,12},{12,16},{16,20},{20,24},{24,28},{1,5},{5,9},{9,... | collective-permute-start | bytes 294920 | tf_op jit(solution)/shard_map/ppermute | solution.py:234
  16.1 1.4 copy.39
  17.8 1.3 copy.40.dec_ref
  19.2 1.2 copy-done.6
  21.4 6.4 %powers.1 = (f32[2048,256]{1,0:T(8,128)S(1)}, f32[2048,256]{1,0:T(8,128)}) custom-call(f32[2048,16]{1,0:T(8,128)S(1)} %copy-done.6, f32[2048,16]{1,0:T(8,128)S(1)} %copy.41.res_ref, bf16[16,256]{1,0:T(8,128)(2,1)S(1)} %copy-done.43, bf16[16,256]{1,0:T(8,128)(2,1)S(1)} %copy-done.32, bf16[256,256]{1,0:T(8,128)(2,1)S(1)} %copy-done.41, ...), custom_call_target="tpu_custom_call" | custom-call | flops 1000000000 | bytes 5000000 | tf_op jit(solution)/shard_map/powers/pallas_call | solution.py:281
  27.8 1.3 copy-done
  30.8 24.2 %near.1 = (bf16[2048,128]{1,0:T(8,128)(2,1)S(1)}, bf16[2048,128]{1,0:T(8,128)(2,1)S(1)}, bf16[2048,128]{1,0:T(8,128)(2,1)S(1)}, f32[2048,128]{1,0:T(8,128)S(1)},...) custom-call(bf16[2048,128]{1,0:T(8,128)(2,1)S(1)} %copy-done.1, ...), custom_call_target="tpu_custom_call" | custom-call | tf_op jit(solution)/shard_map/near/pallas_call | solution.py:293
  58.8 1.3 copy.42.skip_ref
  60.2 39.2 %all-gather.3.cloned.1.call-done = bf16[256,2048]{1,0:T(8,128)(2,1)} async-done(((bf16[32,2048]{1,0:T(8,128)(2,1)}), bf16[256,2048]{1,0:T(8,128)(2,1)}) %all-gather.3.cloned.1.call-update) | async-done | bytes 1048592 | tf_op jit(solution)/shard_map/all_gather | solution.py:303
  99.4 0.9 copy-done.10
  100.3 1.0 copy-done.12
  101.3 1.0 copy-done.14
  104.2 0.9 copy-done.21
  106.7 15.7 %far.1 = (bf16[2048,128]{1,0:T(8,128)(2,1)}, bf16[2048,128]{1,0:T(8,128)(2,1)S(1)}, bf16[2048,128]{1,0:T(8,128)(2,1)S(1)}, bf16[2048,128]{1,0:T(8,128)(2,1)S(1)}...) custom-call(s32[1]{0:T(128)} %bitcast.me_ref, bf16[2048,128]{1,0:T(8,128)(2,1)S(1)} %copy-done.1, ...), custom_call_target="tpu_custom_call" | custom-call | tf_op jit(solution)/shard_map/far/pallas_call | solution.py:306
  126.2 1.3 collective-permute-start.1
  127.5 6.3 %collective-permute-done.1.halo_ref = bf16[24,2048]{1,0:T(8,128)(2,1)S(1)} collective-permute-done((bf16[24,2048]{1,0:T(8,128)(2,1)}, bf16[24,2048]{1,0:T(8,128)(2,1)S(1)}, u32[]{:S(2)}, u32[]{:S(2)}) %collective-permute-start.1) | collective-permute-done | bytes 98336 | tf_op jit(solution)/shard_map/ppermute | solution.py:234
  133.8 1.0 copy-done.34
  134.9 1.0 copy-done.36
  135.9 1.0 copy-done.38
  137.7 13.6 %last.1 = (bf16[2048,128]{1,0:T(8,128)(2,1)}, bf16[2048,128]{1,0:T(8,128)(2,1)}, bf16[2048,128]{1,0:T(8,128)(2,1)}) custom-call(bf16[2048,128]{1,0:T(8,128)(2,1)S(1)} %copy-done.34, bf16[2048,128]{1,0:T(8,128)(2,1)S(1)} %copy-done.36, bf16[2048,128]{1,0:T(8,128)(2,1)S(1)} %copy-done.38, bf16[24,2048]{1,0:T(8,128)(2,1)S(1)} %collective-permute-done.1.halo_ref, ...), custom_call_target="tpu_custom_call" | custom-call | flops 1000000000 | bytes 5000000 | tf_op jit(solution)/shard_map/last/pallas_call | solution.py:321
  151.2 44.8 %all-reduce.2.cloned.1.call-done = f32[40,2048]{1,0:T(8,128)} async-done(((f32[40,2048]{1,0:T(8,128)}), f32[40,2048]{1,0:T(8,128)}) %all-reduce.2.cloned.1.call-update) | async-done | bytes 327696 | tf_op jit(solution)/shard_map/psum | solution.py:320
  196.1 1.0 broadcast_multiply_fusion
  (100 shorter events, 18.0 us)
Async XLA Ops:
  7.2 3.0 %copy-start.3 = (bf16[2048,128]{1,0:T(8,128)(2,1)S(1)}, bf16[2048,128]{1,0:T(8,128)(2,1)}, u32[]{:S(2)}) copy-start(bf16[2048,128]{1,0:T(8,128)(2,1)} %v_ref.3) | copy-start | bytes 1572868
  7.2 92.2 %all-gather.3.cloned.1.call-start = ((), (), s32[]{:S(2)}) async-start(), calls=%async_computation.1 | async-start | bytes 1179648 | tf_op jit(solution)/shard_map/all_gather | solution.py:303
  8.5 7.6 %copy-start.44 = (f32[3,7,2048]{2,1,0:T(8,128)S(1)}, f32[3,7,2048]{2,1,0:T(8,128)}, u32[]{:S(2)}) copy-start(f32[3,7,2048]{2,1,0:T(8,128)} %param.27) | copy-start | bytes 516100
  10.0 7.5 %copy-start.9 = (f32[2048,16]{0,1:T(8,128)S(1)}, f32[2048,16]{0,1:T(8,128)}, u32[]{:S(2)}) copy-start(f32[2048,16]{0,1:T(8,128)} %param.28) | copy-start | bytes 393220
  10.2 7.7 %copy-start.8 = (f32[2048,16]{0,1:T(8,128)S(1)}, f32[2048,16]{0,1:T(8,128)}, u32[]{:S(2)}) copy-start(f32[2048,16]{0,1:T(8,128)} %param.29) | copy-start | bytes 393220
  10.6 8.6 %copy-start.32 = (bf16[16,256]{1,0:T(8,128)(2,1)S(1)}, bf16[16,256]{1,0:T(8,128)(2,1)}, u32[]{:S(2)}) copy-start(bf16[16,256]{1,0:T(8,128)(2,1)} %constant.49.clone.pick_ref) | copy-start | bytes 24580
  10.6 8.6 %copy-start.40 = (bf16[256,256]{1,0:T(8,128)(2,1)S(1)}, bf16[256,256]{1,0:T(8,128)(2,1)}, u32[]{:S(2)}) copy-start(bf16[256,256]{1,0:T(8,128)(2,1)} %constant.41.clone.lo_ref) | copy-start | bytes 393220
  10.6 8.6 %copy-start.43 = (bf16[16,256]{1,0:T(8,128)(2,1)S(1)}, bf16[16,256]{1,0:T(8,128)(2,1)}, u32[]{:S(2)}) copy-start(bf16[16,256]{1,0:T(8,128)(2,1)} %constant.48.clone.times_ref) | copy-start | bytes 24580
  11.2 17.9 %collective-permute-start = (bf16[24,2048]{1,0:T(8,128)(2,1)}, bf16[24,2048]{1,0:T(8,128)(2,1)S(1)}, u32[]{:S(2)}, u32[]{:S(2)}) collective-permute-start(bf16[24,2048]{1,0:T(8,128)(2,1)} %pad_maximum_fusion), channel_id=1, source_target_pairs={{0,4},{4,8},{8,12},{12,16},{16,20},{20,24},{24,28},{1,5},{5,9},{9,... | collective-permute-start | bytes 294920 | tf_op jit(solution)/shard_map/ppermute | solution.py:234
  21.3 8.5 %copy-start.1 = (bf16[2048,128]{1,0:T(8,128)(2,1)S(1)}, bf16[2048,128]{1,0:T(8,128)(2,1)}, u32[]{:S(2)}) copy-start(bf16[2048,128]{1,0:T(8,128)(2,1)} %q_ref.3) | copy-start | bytes 1572868
  21.3 8.5 %copy-start.2 = (bf16[2048,128]{1,0:T(8,128)(2,1)S(1)}, bf16[2048,128]{1,0:T(8,128)(2,1)}, u32[]{:S(2)}) copy-start(bf16[2048,128]{1,0:T(8,128)(2,1)} %k_ref.3) | copy-start | bytes 1572868
  21.3 8.5 %copy-start.5 = (bf16[2048,128]{1,0:T(8,128)(2,1)S(1)}, bf16[2048,128]{1,0:T(8,128)(2,1)}, u32[]{:S(2)}) copy-start(bf16[2048,128]{1,0:T(8,128)(2,1)} %cot_ref.3) | copy-start | bytes 1572868
  21.3 8.5 %copy-start.22 = (bf16[256,256]{1,0:T(8,128)(2,1)S(1)}, bf16[256,256]{1,0:T(8,128)(2,1)}, u32[]{:S(2)}) copy-start(bf16[256,256]{1,0:T(8,128)(2,1)} %constant.45.clone.laglo_ref) | copy-start | bytes 393220
  21.3 8.5 %copy-start.23 = (bf16[256,256]{1,0:T(8,128)(2,1)S(1)}, bf16[256,256]{1,0:T(8,128)(2,1)}, u32[]{:S(2)}) copy-start(bf16[256,256]{1,0:T(8,128)(2,1)} %constant.44.clone.laghi_ref) | copy-start | bytes 393220
  21.3 8.5 %copy-start.24 = (bf16[256,256]{1,0:T(8,128)(2,1)S(1)}, bf16[256,256]{1,0:T(8,128)(2,1)}, u32[]{:S(2)}) copy-start(bf16[256,256]{1,0:T(8,128)(2,1)} %constant.43.clone.back_ref) | copy-start | bytes 393220
  21.3 8.5 %copy-start.25 = (bf16[256,256]{1,0:T(8,128)(2,1)S(1)}, bf16[256,256]{1,0:T(8,128)(2,1)}, u32[]{:S(2)}) copy-start(bf16[256,256]{1,0:T(8,128)(2,1)} %constant.42.clone.mom_ref) | copy-start | bytes 393220
  21.4 8.5 %copy-start.26 = (bf16[256,256]{1,0:T(8,128)(2,1)S(1)}, bf16[256,256]{1,0:T(8,128)(2,1)}, u32[]{:S(2)}) copy-start(bf16[256,256]{1,0:T(8,128)(2,1)} %constant.39.clone.inv_ref) | copy-start | bytes 393220
  21.4 8.5 %copy-start.27 = (bf16[256,256]{1,0:T(8,128)(2,1)S(1)}, bf16[256,256]{1,0:T(8,128)(2,1)}, u32[]{:S(2)}) copy-start(bf16[256,256]{1,0:T(8,128)(2,1)} %constant.38.clone.dft_ref) | copy-start | bytes 393220
  21.4 8.5 %copy-start.30 = (bf16[24,384]{1,0:T(8,128)(2,1)S(1)}, bf16[24,384]{1,0:T(8,128)(2,1)}, u32[]{:S(2)}) copy-start(bf16[24,384]{1,0:T(8,128)(2,1)} %constant.50.clone.place_ref) | copy-start | bytes 55300
  30.8 28.0 %copy-start.45 = (f32[2048]{0:T(1024)S(1)}, f32[2048]{0:T(1024)}, u32[]{:S(2)}) copy-start(f32[2048]{0:T(1024)} %param.30) | copy-start | bytes 24580
  58.0 41.4 %copy-start.7 = (f32[2048,128]{1,0:T(8,128)}, f32[2048,128]{1,0:T(8,128)S(1)}, u32[]{:S(2)}) copy-start(f32[2048,128]{1,0:T(8,128)S(1)} %get-tuple-element.30.near_ref) | copy-start | bytes 3145732
  58.8 137.3 %all-reduce.2.cloned.1.call-start = ((), (), s32[]{:S(2)}) async-start(), calls=%async_computation | async-start | bytes 655360 | tf_op jit(solution)/shard_map/psum | solution.py:320
  106.7 27.1 %copy-start.4 = (f32[21,2048]{0,1:T(8,128)S(1)}, f32[21,2048]{0,1:T(8,128)}, u32[]{:S(2)}) copy-start(f32[21,2048]{0,1:T(8,128)} %copy.39) | copy-start | bytes 516100
  126.2 7.6 %collective-permute-start.1 = (bf16[24,2048]{1,0:T(8,128)(2,1)}, bf16[24,2048]{1,0:T(8,128)(2,1)S(1)}, u32[]{:S(2)}, u32[]{:S(2)}) collective-permute-start(bf16[24,2048]{1,0:T(8,128)(2,1)} %copy-done.39), channel_id=1, source_target_pairs={{4,0},{8,4},{12,8},{16,12},{20,16},{24,20},{28,24},{5,1},{9,5},{13... | collective-permute-start | bytes 294920 | tf_op jit(solution)/shard_map/ppermute | solution.py:234
  (26 other events, 23.0 us)
Sparse Core Ops, SparseCore 0:
  58.9 40.4 all-gather.2
  126.3 69.7 all-reduce.1
where the time goes:
time: 207 us; the launch traced here: 206 us
  waiting for transfers between devices  90.4 us (44%)
  Pallas kernels  59.9 us (29%)
  local copies, waits for them, and re-layouts  32.7 us (16%)
  between operations  14.3 us (7%)
  starting transfers between devices  6.21 us (3%)
  other arithmetic  2.35 us (1%)
    psum x1, waiting for transfers between devices, per_device(): totals = lax.psum(part, 'ctx') * (1.0 / math.sqrt(rows * devices))  44.8 us
    all_gather x1, waiting for transfers between devices, per_device(): every = lax.all_gather(state.astype(BF16), 'ctx')  39.2 us
    unnamed x97, local copies, waits for them, and re-layouts  25.2 us
    pallas_call x1, Pallas kernels, per_device(): pl.pallas_call(functools.partial(near_kernel, taps), grid=grid, in_specs=...  24.2 us
    pallas_call x1, Pallas kernels, per_device(): pl.pallas_call(functools.partial(far_kernel, taps), grid=grid, in_specs=[...  15.7 us
    pallas_call x1, Pallas kernels, per_device(): pl.pallas_call(functools.partial(last_kernel, taps), grid=grid, in_specs=...  13.6 us
    pallas_call x1, Pallas kernels, per_device(): pl.pallas_call(powers_kernel, grid=grid, in_specs=[tall(modes), tall(mode...  6.43 us
    ppermute x2, waiting for transfers between devices, passed_along(): return lax.ppermute(block, axis, route)  6.34 us
  transfers between devices with their start and end apart: 4, of which 3 were waited for; matrix products, arithmetic and copies ran while one was open for 2% of the time, Pallas kernels for 10%

commit v1 on v0

--- a/solution.py
+++ b/solution.py
@@ -149,30 +149,18 @@
     res_ref[...] = folded(powers * moments)
 
 
-def far_kernel(taps, me_ref, q_ref, k_ref, v_ref, cot_ref, halo_ref, qs_ref, ks_ref, vs_ref,
+def far_kernel(taps, q_ref, k_ref, v_ref, cot_ref, halo_ref, qs_ref, ks_ref, vs_ref,
                near_ref, grad_ref, pow_ref, all_ref, state_ref, res_ref, dec_ref, amp_ref, skip_ref,
                place_ref, out_ref, back_ref, pick_ref, sums_ref,
                mixed_ref, gq_ref, gk_ref, gv_ref, head_ref, part_ref):
     rows = q_ref.shape[1]
     lane = lax.broadcasted_iota(jnp.int32, q_ref.shape, 1)
-    me = me_ref[0]
-    count = all_ref.shape[0]
     modes = dec_ref.shape[0]
     dec = dec_ref[...]
     root = jnp.sqrt(2.0 * dec)
     one = jnp.exp(-dec)
-    chunk = jnp.exp(-dec * float(rows))
-    zero = jnp.zeros(dec.shape, F32)
-
-    def ahead(p, s):
-        return jnp.where(p < me, s * chunk + all_ref[p, :modes, :].astype(F32), s)
-
-    def behind(i, r):
-        p = count - 1 - i
-        return jnp.where(p > me, r * chunk + all_ref[p, modes:, :].astype(F32), r)
-
-    s_in = lax.fori_loop(0, count, ahead, zero, unroll=8)
-    r_in = lax.fori_loop(0, count, behind, zero, unroll=8)
+    s_in = all_ref[:modes, :]
+    r_in = all_ref[modes:, :]
     part_ref[:modes, :] = root * (res_ref[...] + one * s_in * state_ref[modes:, :])
     gain = amp_ref[...] * root * one
     powers = pow_ref[...]
@@ -209,7 +197,7 @@
             products.append((values * shifted(x, halo, lane, j)).astype(BF16))
     products.append((gmix * gated).astype(BF16))
     sums = mm(jnp.concatenate(products, 1), sums_ref[...])
-    part_ref[modes:, :] = sums.T[:24, :]
+    part_ref[modes:, :] = sums.T[:32, :]
 
 
 def last_kernel(taps, gq_ref, gk_ref, gv_ref, halo_ref, w_ref, place_ref, oq_ref, ok_ref, ov_ref):
@@ -226,6 +214,75 @@
             at = i * taps + j
             total = total + w[:, at : at + 1] * moved
         out[...] = total.astype(BF16)
+
+
+def partners(axis):
+    n = lax.axis_size(axis)
+    me = lax.axis_index(axis)
+    barrier = pltpu.get_barrier_semaphore()
+    where = [lax.rem(me + d, n) for d in range(n)]
+    for d in range(1, n):
+        pl.semaphore_signal(barrier, inc=1, device_id={axis: where[d]}, device_id_type=pl.DeviceIdType.MESH)
+    pl.semaphore_wait(barrier, n - 1)
+    return n, me, where
+
+
+def send(src, dst, send_sem, recv_sem, axis, target):
+    copy = pltpu.make_async_remote_copy(
+        src_ref=src, dst_ref=dst, send_sem=send_sem, recv_sem=recv_sem,
+        device_id={axis: target}, device_id_type=pl.DeviceIdType.MESH)
+    copy.start()
+    return copy
+
+
+def gather_kernel(rows, state_ref, dec_ref, in_ref, out, got, send_sem, recv_sem):
+    modes = dec_ref.shape[0]
+    out[0] = state_ref[:modes, :].astype(BF16)
+    out[1] = state_ref[modes:, :].astype(BF16)
+    n, me, where = partners("ctx")
+    copies = []
+    for d in range(1, n):
+        kind = jnp.where(where[d] > me, 0, 1)
+        copies.append(send(out.at[kind], got.at[d], send_sem.at[d], recv_sem.at[d], "ctx", where[d]))
+    chunk = jnp.exp(-dec_ref[...] * float(rows))
+    for copy in copies:
+        copy.wait()
+    s = jnp.zeros(chunk.shape, F32)
+    for d in range(n - 1, 0, -1):
+        s = jnp.where(me >= d, s * chunk + got[d].astype(F32), s)
+    in_ref[:modes, :] = s
+    r = jnp.zeros(chunk.shape, F32)
+    for d in range(1, n):
+        r = jnp.where(me < d, r * chunk + got[d].astype(F32), r)
+    in_ref[modes:, :] = r
+
+
+def reduce_kernel(scale, part_ref, head_ref, total_ref, halo_ref, parted, got, mine, full, heads,
+                  send_sem, recv_sem, back_send, back_recv, halo_sem):
+    n = lax.axis_size("ctx")
+    width = parted.shape[2]
+    for p in range(n):
+        parted[p] = part_ref[:, p * width : (p + 1) * width].astype(BF16)
+    n, me, where = partners("ctx")
+    halo = send(head_ref, heads, halo_sem.at[0], halo_sem.at[1], "ctx", where[n - 1])
+    copies = []
+    for d in range(1, n):
+        copies.append(send(parted.at[where[d]], got.at[d], send_sem.at[d], recv_sem.at[d], "ctx", where[d]))
+    total = parted[me].astype(F32)
+    for d in range(1, n):
+        copies[d - 1].wait()
+        total = total + got[d].astype(F32)
+    mine[...] = (total * scale).astype(BF16)
+    copies = []
+    for d in range(1, n):
+        copies.append(send(mine, full.at[d], back_send.at[d], back_recv.at[d], "ctx", where[d]))
+    full[0] = mine[...]
+    halo.wait()
+    halo_ref[...] = jnp.where(me < n - 1, heads[...].astype(F32), 0.0).astype(BF16)
+    for copy in copies:
+        copy.wait()
+    for p in range(n):
+        total_ref[:, p * width : (p + 1) * width] = full[lax.rem(me - p + n, n)].astype(F32)
 
 
 def passed_along(block, axis, distance):
@@ -269,7 +326,7 @@
     def shape(*dims, kind=F32):
         return jax.ShapeDtypeStruct(dims, kind)
 
-    params = pltpu.CompilerParams(vmem_limit_bytes=48 * 1024 * 1024)
+    params = pltpu.CompilerParams(vmem_limit_bytes=60 * 1024 * 1024)
     sent = jnp.concatenate([x[:, rows - 8 :].T for x in (queries, key_signal, value_signal)], 0)
     left = passed_along(sent, "ctx", 1)
     w_tall = short_weight.reshape(3 * taps, channels).T
@@ -300,24 +357,55 @@
         name="near",
     )(queries, key_signal, value_signal, cotangent, left, w_tall, powers, spec, *args)
 
-    every = lax.all_gather(state.astype(BF16), "ctx")
-    me = lax.axis_index("ctx").astype(jnp.int32).reshape(1)
+    dma = pltpu.SemaphoreType.DMA
+    vmem = pl.BlockSpec(memory_space=pltpu.VMEM)
+    every = pl.pallas_call(
+        functools.partial(gather_kernel, rows),
+        in_specs=[vmem] * 2,
+        out_specs=vmem,
+        out_shape=shape(2 * modes, channels),
+        scratch_shapes=[
+            pltpu.VMEM((2, modes, channels), BF16), pltpu.VMEM((devices, modes, channels), BF16),
+            dma((devices,)), dma((devices,)),
+        ],
+        compiler_params=pltpu.CompilerParams(collective_id=0, has_side_effects=True, vmem_limit_bytes=32 * 1024 * 1024),
+        name="gather",
+    )(state, dec_flat)
     args = (tail, tab["out"], tab["out_back"], tab["pick"], sums)
     mixed, gq, gk, gv, heads, part = pl.pallas_call(
         functools.partial(far_kernel, taps),
         grid=grid,
-        in_specs=[pl.BlockSpec(memory_space=pltpu.SMEM)] + [tall(rows)] * 4 + [flat(24)] + [tall(rows)] * 5
-        + [tall(wide), pl.BlockSpec((devices, 2 * modes, block), lambda i: (0, 0, i)), flat(2 * modes), flat(modes), flat(modes), flat(modes), tall(1)]
+        in_specs=[tall(rows)] * 4 + [flat(24)] + [tall(rows)] * 5
+        + [tall(wide), flat(2 * modes), flat(2 * modes), flat(modes), flat(modes), flat(modes), tall(1)]
         + [whole(x) for x in args],
-        out_specs=[tall(rows)] * 4 + [flat(24), flat(modes + 24)],
-        out_shape=[shape(channels, rows, kind=BF16)] * 4 + [shape(24, channels, kind=BF16), shape(modes + 24, channels)],
+        out_specs=[tall(rows)] * 4 + [flat(24), flat(modes + 32)],
+        out_shape=[shape(channels, rows, kind=BF16)] * 4 + [shape(24, channels, kind=BF16), shape(modes + 32, channels)],
         compiler_params=params,
         name="far",
-    )(me, queries, key_signal, value_signal, cotangent, left, q_short, k_short, v_short, near, grad,
+    )(queries, key_signal, value_signal, cotangent, left, q_short, k_short, v_short, near, grad,
       powers, every, state, res, dec_flat, amp_flat, skip, *args)
 
-    right = passed_along(heads, "ctx", -1)
-    totals = lax.psum(part, "ctx") * (1.0 / math.sqrt(rows * devices))
+    scale = 1.0 / math.sqrt(rows * devices)
+    width = channels // devices
+    if width % 128 == 0:
+        height = modes + 32
+        totals, right = pl.pallas_call(
+            functools.partial(reduce_kernel, scale),
+            in_specs=[vmem] * 2,
+            out_specs=[vmem] * 2,
+            out_shape=[shape(height, channels), shape(24, channels, kind=BF16)],
+            scratch_shapes=[
+                pltpu.VMEM((devices, height, width), BF16), pltpu.VMEM((devices, height, width), BF16),
+                pltpu.VMEM((height, width), BF16), pltpu.VMEM((devices, height, width), BF16),
+                pltpu.VMEM((24, channels), BF16),
+                dma((devices,)), dma((devices,)), dma((devices,)), dma((devices,)), dma((2,)),
+            ],
+            compiler_params=pltpu.CompilerParams(collective_id=1, has_side_effects=True, vmem_limit_bytes=32 * 1024 * 1024),
+            name="reduce",
+        )(part, heads)
+    else:
+        right = passed_along(heads, "ctx", -1)
+        totals = lax.psum(part, "ctx") * scale
     grads = pl.pallas_call(
         functools.partial(last_kernel, taps),
         grid=grid,

time: 207 us -> 119 us (0.57)
  waiting for transfers between devices: 90.4 us -> 0.01 us
  Pallas kernels: 59.9 us -> 97.6 us
  local copies, waits for them, and re-layouts: 32.7 us -> 15.6 us
  between operations: 14.3 us -> 0.78 us
  other arithmetic: 2.35 us -> 0.01 us
    psum x1 -> x0, waiting for transfers between devices: 44.8 us -> none  [per_device(): totals = lax.psum(part, 'ctx') * (1.0 / math.sqrt(rows * devices))]
    all_gather x1 -> x0, waiting for transfers between devices: 39.2 us -> none  [per_device(): every = lax.all_gather(state.astype(BF16), 'ctx')]
    pallas_call x0 -> x2, Pallas kernels: none -> 32.3 us  [the longest x1 19.5 us: per_device(): pl.pallas_call(functools.partial(reduce_kernel, scale), in_specs=[vmem] *...]
    unnamed x97 -> x27, local copies, waits for them, and re-layouts: 25.2 us -> 8.06 us
    ppermute x2 -> x1, waiting for transfers between devices: 6.34 us -> 0.01 us  [passed_along(): return lax.ppermute(block, axis, route)]
    pallas_call x1, Pallas kernels: 6.43 us -> 8.7 us  [per_device(): pl.pallas_call(powers_kernel, grid=grid, in_specs=[tall(modes), tall(mode...]
    ppermute x2 -> x1, starting transfers between devices: 6.13 us -> 4.98 us  [passed_along(): return lax.ppermute(block, axis, route)]
  transfers between devices with their start and end apart: 4 -> 1, of which waited for: 3 -> 0; matrix products, arithmetic and copies ran while one was open for 2% -> 5% of each run, Pallas kernels for 10% -> 7%
where the time goes in v1:
time: 119 us
  Pallas kernels  97.6 us (82%)
  local copies, waits for them, and re-layouts  15.6 us (13%)
  starting transfers between devices  4.98 us (4%)
    pallas_call x1, Pallas kernels, per_device(): pl.pallas_call(functools.partial(near_kernel, taps), grid=grid, in_specs=...  25.6 us
    pallas_call x1, Pallas kernels, per_device(): pl.pallas_call(functools.partial(reduce_kernel, scale), in_specs=[vmem] *...  19.5 us
    pallas_call x1, Pallas kernels, per_device(): pl.pallas_call(functools.partial(far_kernel, taps), grid=grid, in_specs=[...  16.3 us
    pallas_call x1, Pallas kernels, per_device(): pl.pallas_call(functools.partial(last_kernel, taps), grid=grid, in_specs=...  14.6 us
    pallas_call x1, Pallas kernels, per_device(): pl.pallas_call(functools.partial(gather_kernel, rows), in_specs=[vmem] *...  12.8 us
    pallas_call x1, Pallas kernels, per_device(): pl.pallas_call(powers_kernel, grid=grid, in_specs=[tall(modes), tall(mode...  8.7 us
    unnamed x27, local copies, waits for them, and re-layouts  8.06 us
    ppermute x1, starting transfers between devices, passed_along(): return lax.ppermute(block, axis, route)  4.98 us
  transfers between devices with their start and end apart: 1, of which 0 were waited for; matrix products, arithmetic and copies ran while one was open for 5% of the time, Pallas kernels for 7%

profile of v1, /device:TPU:0, one launch (start us, length us, event | category | flops | bytes accessed | tf_op | source)
XLA Modules:
  0.0 118.9 jit_solution(15586300907691243354)
XLA Ops:
  0.6 1.3 %slice.18 = bf16[2048,8]{1,0:T(8,128)(2,1)S(1)} slice(bf16[2048,128]{1,0:T(8,128)(2,1)} %q_ref.3), slice={[0:2048], [120:128]} | slice | bytes 65536 | tf_op jit(solution)/shard_map/slice | solution.py:330
  2.0 0.2 copy.43
  2.1 1.3 %slice.19 = bf16[2048,8]{1,0:T(8,128)(2,1)S(1)} slice(bf16[2048,128]{1,0:T(8,128)(2,1)} %k_ref.3), slice={[0:2048], [120:128]} | slice | bytes 65536 | tf_op jit(solution)/shard_map/slice | solution.py:330
  3.6 0.2 slice.20
  4.0 5.0 %collective-permute-start = (bf16[24,2048]{1,0:T(8,128)(2,1)S(1)}, bf16[24,2048]{1,0:T(8,128)(2,1)S(1)}, u32[]{:S(2)}, u32[]{:S(2)}) collective-permute-start(bf16[24,2048]{1,0:T(8,128)(2,1)S(1)} %pad_maximum_fusion), channel_id=1, source_target_pairs={{0,4},{4,8},{8,12},{12,16},{16,20},{20,24},{24,28},{1,5},{5,9},{9,... | collective-permute-start | bytes 294920 | tf_op jit(solution)/shard_map/ppermute | solution.py:291
  9.0 1.4 %copy.39 = f32[21,2048]{0,1:T(8,128)} copy(f32[21,2048]{1,0:T(8,128)S(1)} %reshape.20) | data formatting | bytes 344064 | tf_op jit(solution)/shard_map/reshape | solution.py:332
  10.4 1.4 %copy.42.skip_ref = f32[2048,1]{1,0:T(8,128)} copy(f32[2048,1]{0,1:T(1,128)S(1)} %bitcast.18) | data formatting | bytes 16384 | tf_op jit(solution)/shard_map/broadcast_in_dim | solution.py:335
  11.8 1.4 %copy.41.res_ref = f32[2048,16]{1,0:T(8,128)} copy(f32[2048,16]{0,1:T(8,128)S(1)} %copy-done.7) | data formatting | bytes 262144 | tf_op args[5]
  13.2 1.3 %copy.40.dec_ref = f32[2048,16]{1,0:T(8,128)} copy(f32[2048,16]{0,1:T(8,128)S(1)} %copy-done) | data formatting | bytes 262144 | tf_op args[6]
  14.5 8.7 %powers.1 = (f32[2048,256]{1,0:T(8,128)}, f32[2048,256]{1,0:T(8,128)}) custom-call(f32[2048,16]{1,0:T(8,128)} %copy.40.dec_ref, f32[2048,16]{1,0:T(8,128)} %copy.41.res_ref, bf16[16,256]{1,0:T(8,128)(2,1)} %constant.40.clone.times_ref, bf16[16,256]{1,0:T(8,128)(2,1)} %constant.41.clone.pick_ref, bf16[256,256]{1,0:T(8,128)(2,1)} %constant.32.clone.hi_ref, ...), custom_call_target="tpu_custom_call" | custom-call | flops 1000000000 | bytes 5000000 | tf_op jit(solution)/shard_map/powers/pallas_call | solution.py:338
  23.2 0.6 copy-done.8
  23.9 25.6 %near.1 = (bf16[2048,128]{1,0:T(8,128)(2,1)}, bf16[2048,128]{1,0:T(8,128)(2,1)}, bf16[2048,128]{1,0:T(8,128)(2,1)}, f32[2048,128]{1,0:T(8,128)}, f32[2048,128]{1...) custom-call(bf16[2048,128]{1,0:T(8,128)(2,1)} %q_ref.3, bf16[2048,128]{1,0:T(8,128)(2,1)} %k_ref.3, ...), custom_call_target="tpu_custom_call" | custom-call | tf_op jit(solution)/shard_map/near/pallas_call | solution.py:350
  49.5 0.9 copy-done.1
  50.5 12.8 %gather.1.all_ref = f32[32,2048]{1,0:T(8,128)S(1)} custom-call(f32[32,2048]{1,0:T(8,128)S(1)} %copy-done.1, f32[16,2048]{1,0:T(8,128)S(1)} %bitcast.11), custom_call_target="tpu_custom_call" | custom-call | tf_op jit(solution)/shard_map/gather/pallas_call | solution.py:362
  63.3 0.7 copy-done.2
  64.0 16.3 %far.1 = (bf16[2048,128]{1,0:T(8,128)(2,1)}, bf16[2048,128]{1,0:T(8,128)(2,1)}, bf16[2048,128]{1,0:T(8,128)(2,1)}, bf16[2048,128]{1,0:T(8,128)(2,1)}, bf16[24,2048]{1,0:T(8,128)(2,1)}, /*index=5*/f32[48,2048]{1,0:T(8,128)}) custom-call(bf16[2048,128]{1,0:T(8,128)(2,1)} %q_ref.3, bf16[2048,128]{1,0:T(8,128)(2,1)} %k_ref.3, bf16[2048,128]{1,0:T(8,128)(2,1)} %v_ref.3, ...), custom_call_target="tpu_custom_call" | custom-call | tf_op jit(solution)/shard_map/far/pallas_call | solution.py:375
  80.3 1.0 copy-done.3
  81.3 0.9 copy-done.4
  82.2 19.5 %reduce.1 = (f32[48,2048]{1,0:T(8,128)S(1)}, bf16[24,2048]{1,0:T(8,128)(2,1)S(1)}) custom-call(f32[48,2048]{1,0:T(8,128)S(1)} %copy-done.3, bf16[24,2048]{1,0:T(8,128)(2,1)S(1)} %copy-done.4), custom_call_target="tpu_custom_call" | custom-call | tf_op jit(solution)/shard_map/reduce/pallas_call | solution.py:392
  101.7 0.6 copy-done.5
  102.3 0.6 slice.23
  102.9 0.7 slice_bitcast_fusion
  103.6 0.7 reshape.21
  104.3 14.6 %last.1 = (bf16[2048,128]{1,0:T(8,128)(2,1)}, bf16[2048,128]{1,0:T(8,128)(2,1)}, bf16[2048,128]{1,0:T(8,128)(2,1)}) custom-call(bf16[2048,128]{1,0:T(8,128)(2,1)} %get-tuple-element.37.gq_ref, bf16[2048,128]{1,0:T(8,128)(2,1)} %get-tuple-element.38.gk_ref, bf16[2048,128]{1,0:T(8,128)(2,1)} %get-tuple-element.39.gv_ref, bf16[24,2048]{1,0:T(8,128)(2,1)} %copy-done.5, ...), custom_call_target="tpu_custom_call" | custom-call | flops 1000000000 | bytes 5000000 | tf_op jit(solution)/shard_map/last/pallas_call | solution.py:409
  (22 shorter events, 0.4 us)
Async XLA Ops:
  0.6 3.0 %copy-start.6 = (bf16[2048,128]{1,0:T(8,128)(2,1)S(1)}, bf16[2048,128]{1,0:T(8,128)(2,1)}, u32[]{:S(2)}) copy-start(bf16[2048,128]{1,0:T(8,128)(2,1)} %v_ref.3) | copy-start | bytes 1572868
  2.0 7.0 %copy-start.9 = (f32[3,7,2048]{2,1,0:T(8,128)S(1)}, f32[3,7,2048]{2,1,0:T(8,128)}, u32[]{:S(2)}) copy-start(f32[3,7,2048]{2,1,0:T(8,128)} %param.27) | copy-start | bytes 516100
  3.4 7.0 %copy-start.10 = (f32[2048]{0:T(1024)S(1)}, f32[2048]{0:T(1024)}, u32[]{:S(2)}) copy-start(f32[2048]{0:T(1024)} %param.30) | copy-start | bytes 24580
  3.6 8.2 %copy-start.7 = (f32[2048,16]{0,1:T(8,128)S(1)}, f32[2048,16]{0,1:T(8,128)}, u32[]{:S(2)}) copy-start(f32[2048,16]{0,1:T(8,128)} %param.28) | copy-start | bytes 393220
  4.0 9.2 %copy-start = (f32[2048,16]{0,1:T(8,128)S(1)}, f32[2048,16]{0,1:T(8,128)}, u32[]{:S(2)}) copy-start(f32[2048,16]{0,1:T(8,128)} %param.29) | copy-start | bytes 393220
  4.0 19.2 %collective-permute-start = (bf16[24,2048]{1,0:T(8,128)(2,1)S(1)}, bf16[24,2048]{1,0:T(8,128)(2,1)S(1)}, u32[]{:S(2)}, u32[]{:S(2)}) collective-permute-start(bf16[24,2048]{1,0:T(8,128)(2,1)S(1)} %pad_maximum_fusion), channel_id=1, source_target_pairs={{0,4},{4,8},{8,12},{12,16},{16,20},{20,24},{24,28},{1,5},{5,9},{9,... | collective-permute-start | bytes 294920 | tf_op jit(solution)/shard_map/ppermute | solution.py:291
  23.2 0.6 copy-start.8
  49.5 1.0 copy-start.1
  63.3 0.7 copy-start.2
  80.3 1.0 copy-start.3
  81.3 0.9 copy-start.4
  101.7 0.6 copy-start.5

commit v2 on v1

--- a/solution.py
+++ b/solution.py
@@ -83,8 +83,11 @@
     return total
 
 
-def powers_kernel(dec_ref, res_ref, times_ref, pick_ref, hi_ref, lo_ref, pow_ref, spec_ref):
+def powers_kernel(dec_ref, res_ref, times_ref, pick_ref, hi_ref, lo_ref, eye_ref, pow_ref, spec_ref, flat_ref):
     dec = dec_ref[...]
+    modes = dec.shape[1]
+    flat_ref[:modes, :] = exact(lambda x, eye: mm_nt(eye, x), dec, eye_ref[...], 3)
+    flat_ref[modes:, :] = exact(lambda x, eye: mm_nt(eye, x), res_ref[...], eye_ref[...], 3)
     gain = res_ref[...] * jnp.sqrt(2.0 * dec)
     powers = jnp.exp(-exact(mm, dec, times_ref[...], 3))
     pow_ref[...] = powers
@@ -92,29 +95,33 @@
     spec_ref[...] = mm(high, hi_ref[...]) + mm(low, hi_ref[...]) + mm(high, lo_ref[...])
 
 
-def shifted(x, halo, lane, j):
-    rows = x.shape[1]
-    if j == 0:
-        return x
-    return pltpu.roll(jnp.where(lane >= rows - j, halo, x), j, 1)
+def moved(x, halo, table):
+    return mm(jnp.concatenate([x, halo.astype(BF16)], 1), table)
+
+
+def weights_wide(w_ref, wide_ref):
+    return mm_tn(jnp.concatenate(parts(w_ref[...], 3), 0), wide_ref[...])
+
+
+def tap_sum(shifts, w, i, taps, rows):
+    total = None
+    for j in range(taps):
+        at = (i * taps + j) * rows
+        term = w[:, at : at + rows] * shifts[:, j * rows : (j + 1) * rows]
+        total = term if total is None else total + term
+    return total
 
 
 def near_kernel(taps, q_ref, k_ref, v_ref, cot_ref, halo_ref, w_ref, pow_ref, spec_ref,
-                place_ref, dft_ref, inv_ref, mom_ref, back_ref, laghi_ref, laglo_ref, pick_ref,
+                place_ref, shift_ref, wide_ref, dft_ref, inv_ref, mom_ref, back_ref, laghi_ref, laglo_ref, pick_ref,
                 qs_ref, ks_ref, vs_ref, near_ref, grad_ref, state_ref, res_ref):
     rows = q_ref.shape[1]
-    lane = lax.broadcasted_iota(jnp.int32, q_ref.shape, 1)
     halos = mm_tn(halo_ref[...], place_ref[...])
-    w = w_ref[...]
+    w = weights_wide(w_ref, wide_ref)
     short = []
     for i, ref in enumerate((q_ref, k_ref, v_ref)):
-        x = ref[...].astype(F32)
-        halo = halos[:, i * rows : (i + 1) * rows]
-        total = jnp.zeros(x.shape, F32)
-        for j in range(taps):
-            at = i * taps + j
-            total = total + w[:, at : at + 1] * shifted(x, halo, lane, j)
-        short.append(total.astype(BF16))
+        shifts = moved(ref[...], halos[:, i * rows : (i + 1) * rows], shift_ref[...])
+        short.append(tap_sum(shifts, w, i, taps, rows).astype(BF16))
     qs_ref[...], ks_ref[...], vs_ref[...] = short
     gated = (short[1].astype(F32) * short[2].astype(F32)).astype(BF16)
     gmix = (cot_ref[...].astype(F32) * short[0].astype(F32)).astype(BF16)
@@ -151,10 +158,9 @@
 
 def far_kernel(taps, q_ref, k_ref, v_ref, cot_ref, halo_ref, qs_ref, ks_ref, vs_ref,
                near_ref, grad_ref, pow_ref, all_ref, state_ref, res_ref, dec_ref, amp_ref, skip_ref,
-               place_ref, out_ref, back_ref, pick_ref, sums_ref,
+               place_ref, shift_ref, ones_ref, out_ref, back_ref, pick_ref, sums_ref,
                mixed_ref, gq_ref, gk_ref, gv_ref, head_ref, part_ref):
     rows = q_ref.shape[1]
-    lane = lax.broadcasted_iota(jnp.int32, q_ref.shape, 1)
     modes = dec_ref.shape[0]
     dec = dec_ref[...]
     root = jnp.sqrt(2.0 * dec)
@@ -173,7 +179,7 @@
 
     conv = (near_ref[...] + spread(gain * s_in, out_ref)).astype(BF16)
     gconv = (grad_ref[...] + spread(gain * r_in, back_ref)).astype(BF16)
-    skip = skip_ref[...]
+    skip = exact(mm_tn, skip_ref[...], ones_ref[...], 3)
     qs, ks, vs = qs_ref[...].astype(F32), ks_ref[...].astype(F32), vs_ref[...].astype(F32)
     cot = cot_ref[...].astype(F32)
     gated = (ks * vs).astype(BF16).astype(F32)
@@ -190,30 +196,22 @@
     halos = mm_tn(halo_ref[...], place_ref[...])
     products = []
     for i, (ref, grads) in enumerate(((q_ref, gq), (k_ref, gk), (v_ref, gv))):
-        x = ref[...].astype(F32)
         values = grads.astype(F32)
-        halo = halos[:, i * rows : (i + 1) * rows]
+        shifts = moved(ref[...], halos[:, i * rows : (i + 1) * rows], shift_ref[...])
         for j in range(taps):
-            products.append((values * shifted(x, halo, lane, j)).astype(BF16))
+            products.append((values * shifts[:, j * rows : (j + 1) * rows]).astype(BF16))
     products.append((gmix * gated).astype(BF16))
     sums = mm(jnp.concatenate(products, 1), sums_ref[...])
     part_ref[modes:, :] = sums.T[:32, :]
 
 
-def last_kernel(taps, gq_ref, gk_ref, gv_ref, halo_ref, w_ref, place_ref, oq_ref, ok_ref, ov_ref):
+def last_kernel(taps, gq_ref, gk_ref, gv_ref, halo_ref, w_ref, place_ref, shift_ref, wide_ref, oq_ref, ok_ref, ov_ref):
     rows = gq_ref.shape[1]
-    lane = lax.broadcasted_iota(jnp.int32, gq_ref.shape, 1)
     halos = mm_tn(halo_ref[...], place_ref[...])
-    w = w_ref[...]
+    w = weights_wide(w_ref, wide_ref)
     for i, (ref, out) in enumerate(((gq_ref, oq_ref), (gk_ref, ok_ref), (gv_ref, ov_ref))):
-        x = ref[...].astype(F32)
-        halo = halos[:, i * rows : (i + 1) * rows]
-        total = jnp.zeros(x.shape, F32)
-        for j in range(taps):
-            moved = x if j == 0 else pltpu.roll(jnp.where(lane < j, halo, x), rows - j, 1)
-            at = i * taps + j
-            total = total + w[:, at : at + 1] * moved
-        out[...] = total.astype(BF16)
+        shifts = moved(ref[...], halos[:, i * rows : (i + 1) * rows], shift_ref[...])
+        out[...] = tap_sum(shifts, w, i, taps, rows).astype(BF16)
 
 
 def partners(axis):
@@ -235,8 +233,24 @@
     return copy
 
 
+def halo_kernel(q_ref, k_ref, v_ref, halo_ref, tails, got, sems):
+    rows = q_ref.shape[1]
+    shape = (8, rows)
+    last = (lax.broadcasted_iota(jnp.int32, shape, 0) + (rows - 8) == lax.broadcasted_iota(jnp.int32, shape, 1)).astype(BF16)
+    tails[...] = jnp.concatenate([mm_nt(last, ref[...]) for ref in (q_ref, k_ref, v_ref)], 0).astype(BF16)
+    n = lax.axis_size("ctx")
+    me = lax.axis_index("ctx")
+    right, left = lax.rem(me + 1, n), lax.rem(me + n - 1, n)
+    barrier = pltpu.get_barrier_semaphore()
+    for other in (right, left):
+        pl.semaphore_signal(barrier, inc=1, device_id={"ctx": other}, device_id_type=pl.DeviceIdType.MESH)
+    pl.semaphore_wait(barrier, 2)
+    send(tails, got, sems.at[0], sems.at[1], "ctx", right).wait()
+    halo_ref[...] = jnp.where(me > 0, got[...].astype(F32), 0.0).astype(BF16)
+
+
 def gather_kernel(rows, state_ref, dec_ref, in_ref, out, got, send_sem, recv_sem):
-    modes = dec_ref.shape[0]
+    modes = dec_ref.shape[0] // 2
     out[0] = state_ref[:modes, :].astype(BF16)
     out[1] = state_ref[modes:, :].astype(BF16)
     n, me, where = partners("ctx")
@@ -244,7 +258,7 @@
     for d in range(1, n):
         kind = jnp.where(where[d] > me, 0, 1)
         copies.append(send(out.at[kind], got.at[d], send_sem.at[d], recv_sem.at[d], "ctx", where[d]))
-    chunk = jnp.exp(-dec_ref[...] * float(rows))
+    chunk = jnp.exp(-dec_ref[:modes, :] * float(rows))
     for copy in copies:
         copy.wait()
     s = jnp.zeros(chunk.shape, F32)
@@ -327,38 +341,53 @@
         return jax.ShapeDtypeStruct(dims, kind)
 
     params = pltpu.CompilerParams(vmem_limit_bytes=60 * 1024 * 1024)
-    sent = jnp.concatenate([x[:, rows - 8 :].T for x in (queries, key_signal, value_signal)], 0)
-    left = passed_along(sent, "ctx", 1)
-    w_tall = short_weight.reshape(3 * taps, channels).T
-    dec_flat = decay_rates.T
-    amp_flat = residues.T
-    skip = skip_gain[:, None]
-
-    args = (tab["times"], tab["pick"], tab["spec_hi"], tab["spec_lo"])
-    powers, spec = pl.pallas_call(
+    dma = pltpu.SemaphoreType.DMA
+    vmem = pl.BlockSpec(memory_space=pltpu.VMEM)
+    left = pl.pallas_call(
+        halo_kernel,
+        in_specs=[vmem] * 3,
+        out_specs=vmem,
+        out_shape=shape(24, channels, kind=BF16),
+        scratch_shapes=[pltpu.VMEM((24, channels), BF16)] * 2 + [dma((2,))],
+        compiler_params=pltpu.CompilerParams(collective_id=2, has_side_effects=True, vmem_limit_bytes=60 * 1024 * 1024),
+        name="halo",
+    )(queries, key_signal, value_signal)
+    w_flat = jnp.concatenate([short_weight.reshape(3 * taps, channels), jnp.zeros((24 - 3 * taps, channels), F32)], 0)
+    skip = skip_gain[None, :]
+    both = [np.zeros((2 * rows, taps * rows), np.float32) for _ in range(2)]
+    for j in range(taps):
+        for t in range(rows):
+            both[0][t - j if t >= j else 2 * rows + t - j, j * rows + t] = 1
+            both[1][t + j, j * rows + t] = 1
+    before, after = (jnp.asarray(x, BF16) for x in both)
+    spread_w = np.zeros((24, 3 * taps * rows), np.float32)
+    for i in range(3 * taps):
+        spread_w[i, i * rows : (i + 1) * rows] = 1
+    spread_w = jnp.asarray(np.tile(spread_w, (3, 1)), BF16)
+
+    args = (tab["times"], tab["pick"], tab["spec_hi"], tab["spec_lo"], jnp.eye(modes, dtype=BF16))
+    powers, spec, flats = pl.pallas_call(
         powers_kernel,
         grid=grid,
         in_specs=[tall(modes), tall(modes)] + [whole(x) for x in args],
-        out_specs=[tall(wide), tall(2 * rows)],
-        out_shape=[shape(channels, wide), shape(channels, 2 * rows)],
+        out_specs=[tall(wide), tall(2 * rows), flat(2 * modes)],
+        out_shape=[shape(channels, wide), shape(channels, 2 * rows), shape(2 * modes, channels)],
         compiler_params=params,
         cost_estimate=pl.CostEstimate(flops=10**9, bytes_accessed=5 * 10**6, transcendentals=10**6),
         name="powers",
     )(decay_rates, residues, *args)
 
-    args = (tail, tab["dft"], tab["inv"], tab["mom"], tab["mom_back"], tab["lag_hi"], tab["lag_lo"], tab["pick"])
+    args = (tail, before, spread_w, tab["dft"], tab["inv"], tab["mom"], tab["mom_back"], tab["lag_hi"], tab["lag_lo"], tab["pick"])
     q_short, k_short, v_short, near, grad, state, res = pl.pallas_call(
         functools.partial(near_kernel, taps),
         grid=grid,
-        in_specs=[tall(rows)] * 4 + [flat(24), tall(3 * taps), tall(wide), tall(2 * rows)] + [whole(x) for x in args],
+        in_specs=[tall(rows)] * 4 + [flat(24), flat(24), tall(wide), tall(2 * rows)] + [whole(x) for x in args],
         out_specs=[tall(rows)] * 5 + [flat(2 * modes), flat(modes)],
         out_shape=[shape(channels, rows, kind=BF16)] * 3 + [shape(channels, rows)] * 2 + [shape(2 * modes, channels), shape(modes, channels)],
         compiler_params=params,
         name="near",
-    )(queries, key_signal, value_signal, cotangent, left, w_tall, powers, spec, *args)
-
-    dma = pltpu.SemaphoreType.DMA
-    vmem = pl.BlockSpec(memory_space=pltpu.VMEM)
+    )(queries, key_signal, value_signal, cotangent, left, w_flat, powers, spec, *args)
+
     every = pl.pallas_call(
         functools.partial(gather_kernel, rows),
         in_specs=[vmem] * 2,
@@ -368,22 +397,22 @@
             pltpu.VMEM((2, modes, channels), BF16), pltpu.VMEM((devices, modes, channels), BF16),
             dma((devices,)), dma((devices,)),
         ],
-        compiler_params=pltpu.CompilerParams(collective_id=0, has_side_effects=True, vmem_limit_bytes=32 * 1024 * 1024),
+        compiler_params=pltpu.CompilerParams(collective_id=0, has_side_effects=True, vmem_limit_bytes=60 * 1024 * 1024),
         name="gather",
-    )(state, dec_flat)
-    args = (tail, tab["out"], tab["out_back"], tab["pick"], sums)
+    )(state, flats)
+    args = (tail, before, jnp.ones((1, rows), BF16), tab["out"], tab["out_back"], tab["pick"], sums)
     mixed, gq, gk, gv, heads, part = pl.pallas_call(
         functools.partial(far_kernel, taps),
         grid=grid,
         in_specs=[tall(rows)] * 4 + [flat(24)] + [tall(rows)] * 5
-        + [tall(wide), flat(2 * modes), flat(2 * modes), flat(modes), flat(modes), flat(modes), tall(1)]
+        + [tall(wide), flat(2 * modes), flat(2 * modes), flat(modes), flat(modes), pl.BlockSpec((modes, block), lambda i: (1, i)), flat(1)]
         + [whole(x) for x in args],
         out_specs=[tall(rows)] * 4 + [flat(24), flat(modes + 32)],
         out_shape=[shape(channels, rows, kind=BF16)] * 4 + [shape(24, channels, kind=BF16), shape(modes + 32, channels)],
         compiler_params=params,
         name="far",
     )(queries, key_signal, value_signal, cotangent, left, q_short, k_short, v_short, near, grad,
-      powers, every, state, res, dec_flat, amp_flat, skip, *args)
+      powers, every, state, res, flats, flats, skip, *args)
 
     scale = 1.0 / math.sqrt(rows * devices)
     width = channels // devices
@@ -400,7 +429,7 @@
                 pltpu.VMEM((24, channels), BF16),
                 dma((devices,)), dma((devices,)), dma((devices,)), dma((devices,)), dma((2,)),
             ],
-            compiler_params=pltpu.CompilerParams(collective_id=1, has_side_effects=True, vmem_limit_bytes=32 * 1024 * 1024),
+            compiler_params=pltpu.CompilerParams(collective_id=1, has_side_effects=True, vmem_limit_bytes=60 * 1024 * 1024),
             name="reduce",
         )(part, heads)
     else:
@@ -409,13 +438,13 @@
     grads = pl.pallas_call(
         functools.partial(last_kernel, taps),
         grid=grid,
-        in_specs=[tall(rows)] * 3 + [flat(24), tall(3 * taps), whole(head)],
+        in_specs=[tall(rows)] * 3 + [flat(24), flat(24), whole(head), whole(after), whole(spread_w)],
         out_specs=[tall(rows)] * 3,
         out_shape=[shape(channels, rows, kind=BF16)] * 3,
         compiler_params=params,
         cost_estimate=pl.CostEstimate(flops=10**9, bytes_accessed=5 * 10**6, transcendentals=0),
         name="last",
-    )(gq, gk, gv, right, w_tall, head)
+    )(gq, gk, gv, right, w_flat, head, after, spread_w)
     return (
         mixed,
         *grads,

time: 119 us -> 109 us (0.916)
  local copies, waits for them, and re-layouts: 15.6 us -> 6.82 us
  starting transfers between devices: 4.98 us -> 0 us
  Pallas kernels: 97.6 us -> 101 us
    pallas_call x0 -> x1, Pallas kernels: none -> 11.7 us  [per_device(): pl.pallas_call(halo_kernel, in_specs=[vmem] * 3, out_specs=vmem, out_shap...]
    pallas_call x1, Pallas kernels: 25.6 us -> 18.2 us  [per_device(): pl.pallas_call(functools.partial(near_kernel, taps), grid=grid, in_specs=...]
    unnamed x27 -> x8, local copies, waits for them, and re-layouts: 8.06 us -> 2.67 us
    ppermute x1 -> x0, starting transfers between devices: 4.98 us -> none  [passed_along(): return lax.ppermute(block, axis, route)]
    pallas_call x1, Pallas kernels: 14.6 us -> 10.5 us  [per_device(): pl.pallas_call(functools.partial(last_kernel, taps), grid=grid, in_specs=...]
    slice x3 -> x0, local copies, waits for them, and re-layouts: 2.78 us -> none  [per_device(): x[:, rows - 8:]]
  transfers between devices with their start and end apart: 1 -> 0, of which waited for: 0 -> 0; matrix products, arithmetic and copies ran while one was open for 5% -> 0% of each run, Pallas kernels for 7% -> 0%
where the time goes in v2:
time: 109 us
  Pallas kernels  101 us (93%)
  local copies, waits for them, and re-layouts  6.82 us (6%)
    pallas_call x1, Pallas kernels, per_device(): pl.pallas_call(functools.partial(reduce_kernel, scale), in_specs=[vmem] *...  20.7 us
    pallas_call x1, Pallas kernels, per_device(): pl.pallas_call(functools.partial(near_kernel, taps), grid=grid, in_specs=...  18.2 us
    pallas_call x1, Pallas kernels, per_device(): pl.pallas_call(functools.partial(far_kernel, taps), grid=grid, in_specs=[...  17 us
    pallas_call x1, Pallas kernels, per_device(): pl.pallas_call(functools.partial(gather_kernel, rows), in_specs=[vmem] *...  13.5 us
    pallas_call x1, Pallas kernels, per_device(): pl.pallas_call(halo_kernel, in_specs=[vmem] * 3, out_specs=vmem, out_shap...  11.7 us
    pallas_call x1, Pallas kernels, per_device(): pl.pallas_call(functools.partial(last_kernel, taps), grid=grid, in_specs=...  10.5 us
    pallas_call x1, Pallas kernels, per_device(): pl.pallas_call(powers_kernel, grid=grid, in_specs=[tall(modes), tall(mode...  9.23 us
    unnamed x8, local copies, waits for them, and re-layouts  2.67 us

profile of v2, /device:TPU:0, one launch (start us, length us, event | category | flops | bytes accessed | tf_op | source)
XLA Modules:
  0.0 108.9 jit_solution(16554733538248421415)
XLA Ops:
  0.6 0.0 copy-start.2
  0.6 0.0 copy-start.1
  0.7 0.6 fusion.eye_ref
  1.3 11.7 %halo.1.halo_ref = bf16[24,2048]{1,0:T(8,128)(2,1)} custom-call(bf16[2048,128]{1,0:T(8,128)(2,1)} %q_ref.5, bf16[2048,128]{1,0:T(8,128)(2,1)} %k_ref.5, bf16[2048,128]{1,0:T(8,128)(2,1)} %v_ref.5), custom_call_target="tpu_custom_call" | custom-call | tf_op jit(solution)/shard_map/halo/pallas_call | solution.py:346
  12.9 1.0 reshape.20
  13.9 0.7 concatenate.3.w_ref
  14.6 0.0 copy-done.1
  14.6 1.4 %copy.34.res_ref = f32[2048,16]{1,0:T(8,128)} copy(f32[2048,16]{0,1:T(8,128)S(1)} %copy-done.1) | data formatting | bytes 262144 | tf_op args[5]
  15.9 0.0 copy-done.2
  15.9 1.3 %copy.33.dec_ref = f32[2048,16]{1,0:T(8,128)} copy(f32[2048,16]{0,1:T(8,128)S(1)} %copy-done.2) | data formatting | bytes 262144 | tf_op args[6]
  17.2 9.2 %powers.1 = (f32[2048,256]{1,0:T(8,128)}, f32[2048,256]{1,0:T(8,128)}, f32[32,2048]{1,0:T(8,128)}) custom-call(f32[2048,16]{1,0:T(8,128)} %copy.33.dec_ref, f32[2048,16]{1,0:T(8,128)} %copy.34.res_ref, bf16[16,256]{1,0:T(8,128)(2,1)} %constant.50.clone.times_ref, bf16[16,256]{1,0:T(8,128)(2,1)} %constant.51.clone.pick_ref, ...), custom_call_target="tpu_custom_call" | custom-call | flops 1000000000 | bytes 5000000 | tf_op jit(solution)/shard_map/powers/pallas_call | solution.py:369
  26.5 18.2 %near.1 = (bf16[2048,128]{1,0:T(8,128)(2,1)}, bf16[2048,128]{1,0:T(8,128)(2,1)}, bf16[2048,128]{1,0:T(8,128)(2,1)}, f32[2048,128]{1,0:T(8,128)}, f32[2048,128]{1...) custom-call(bf16[2048,128]{1,0:T(8,128)(2,1)} %q_ref.5, bf16[2048,128]{1,0:T(8,128)(2,1)} %k_ref.5, ...), custom_call_target="tpu_custom_call" | custom-call | tf_op jit(solution)/shard_map/near/pallas_call | solution.py:381
  44.7 13.5 %gather.1.all_ref = f32[32,2048]{1,0:T(8,128)} custom-call(f32[32,2048]{1,0:T(8,128)} %get-tuple-element.35.state_ref, f32[32,2048]{1,0:T(8,128)} %get-tuple-element.36.dec_ref.amp_ref), custom_call_target="tpu_custom_call" | custom-call | tf_op jit(solution)/shard_map/gather/pallas_call | solution.py:391
  58.2 0.5 broadcast_in_dim.8.ones_ref
  58.7 17.0 %far.1 = (bf16[2048,128]{1,0:T(8,128)(2,1)}, bf16[2048,128]{1,0:T(8,128)(2,1)}, bf16[2048,128]{1,0:T(8,128)(2,1)}, bf16[2048,128]{1,0:T(8,128)(2,1)}, bf16[24,2048]{1,0:T(8,128)(2,1)}, /*index=5*/f32[48,2048]{1,0:T(8,128)}) custom-call(bf16[2048,128]{1,0:T(8,128)(2,1)} %q_ref.5, bf16[2048,128]{1,0:T(8,128)(2,1)} %k_ref.5, bf16[2048,128]{1,0:T(8,128)(2,1)} %v_ref.5, ...), custom_call_target="tpu_custom_call" | custom-call | tf_op jit(solution)/shard_map/far/pallas_call | solution.py:404
  75.7 20.7 %reduce.1 = (f32[48,2048]{1,0:T(8,128)}, bf16[24,2048]{1,0:T(8,128)(2,1)}) custom-call(f32[48,2048]{1,0:T(8,128)} %get-tuple-element.42.part_ref, bf16[24,2048]{1,0:T(8,128)(2,1)} %get-tuple-element.43.head_ref), custom_call_target="tpu_custom_call" | custom-call | tf_op jit(solution)/shard_map/reduce/pallas_call | solution.py:421
  96.4 0.0 copy-start
  96.4 10.5 %last.1 = (bf16[2048,128]{1,0:T(8,128)(2,1)}, bf16[2048,128]{1,0:T(8,128)(2,1)}, bf16[2048,128]{1,0:T(8,128)(2,1)}) custom-call(bf16[2048,128]{1,0:T(8,128)(2,1)} %get-tuple-element.39.gq_ref, bf16[2048,128]{1,0:T(8,128)(2,1)} %get-tuple-element.40.gk_ref, bf16[2048,128]{1,0:T(8,128)(2,1)} %get-tuple-element.41.gv_ref, ...), custom_call_target="tpu_custom_call" | custom-call | flops 1000000000 | bytes 5000000 | tf_op jit(solution)/shard_map/last/pallas_call | solution.py:438
  106.9 0.0 copy-done
  106.9 0.6 slice.11
  107.5 0.7 slice_bitcast_fusion
  108.2 0.7 reshape.21
  (1 shorter events, 0.0 us)
Async XLA Ops:
  0.6 15.3 %copy-start.2 = (f32[2048,16]{0,1:T(8,128)S(1)}, f32[2048,16]{0,1:T(8,128)}, u32[]{:S(2)}) copy-start(f32[2048,16]{0,1:T(8,128)} %param.32) | copy-start | bytes 393220
  0.6 13.9 %copy-start.1 = (f32[2048,16]{0,1:T(8,128)S(1)}, f32[2048,16]{0,1:T(8,128)}, u32[]{:S(2)}) copy-start(f32[2048,16]{0,1:T(8,128)} %param.31) | copy-start | bytes 393220
  96.4 10.5 %copy-start = (f32[48,2048]{1,0:T(8,128)S(1)}, f32[48,2048]{1,0:T(8,128)}, u32[]{:S(2)}) copy-start(f32[48,2048]{1,0:T(8,128)} %get-tuple-element.48) | copy-start | bytes 1179652

commit v3 on v2

--- a/solution.py
+++ b/solution.py
@@ -205,13 +205,20 @@
     part_ref[modes:, :] = sums.T[:32, :]
 
 
+def anti_taps(taps, grads, halo, w, place_ref, shift_ref, wide_ref):
+    rows = grads[0].shape[1]
+    halos = mm_tn(halo, place_ref[...])
+    w = mm_tn(jnp.concatenate(parts(w, 3), 0), wide_ref[...])
+    outs = []
+    for i, x in enumerate(grads):
+        shifts = moved(x, halos[:, i * rows : (i + 1) * rows], shift_ref[...])
+        outs.append(tap_sum(shifts, w, i, taps, rows).astype(BF16))
+    return outs
+
+
 def last_kernel(taps, gq_ref, gk_ref, gv_ref, halo_ref, w_ref, place_ref, shift_ref, wide_ref, oq_ref, ok_ref, ov_ref):
-    rows = gq_ref.shape[1]
-    halos = mm_tn(halo_ref[...], place_ref[...])
-    w = weights_wide(w_ref, wide_ref)
-    for i, (ref, out) in enumerate(((gq_ref, oq_ref), (gk_ref, ok_ref), (gv_ref, ov_ref))):
-        shifts = moved(ref[...], halos[:, i * rows : (i + 1) * rows], shift_ref[...])
-        out[...] = tap_sum(shifts, w, i, taps, rows).astype(BF16)
+    oq_ref[...], ok_ref[...], ov_ref[...] = anti_taps(
+        taps, (gq_ref[...], gk_ref[...], gv_ref[...]), halo_ref[...], w_ref[...], place_ref, shift_ref, wide_ref)
 
 
 def partners(axis):
@@ -233,20 +240,33 @@
     return copy
 
 
-def halo_kernel(q_ref, k_ref, v_ref, halo_ref, tails, got, sems):
+def first_kernel(dec_ref, res_ref, times_ref, pick_ref, hi_ref, lo_ref, eye_ref, q_ref, k_ref, v_ref,
+                 pow_ref, spec_ref, flat_ref, halo_ref, tails, got, sems):
     rows = q_ref.shape[1]
-    shape = (8, rows)
-    last = (lax.broadcasted_iota(jnp.int32, shape, 0) + (rows - 8) == lax.broadcasted_iota(jnp.int32, shape, 1)).astype(BF16)
-    tails[...] = jnp.concatenate([mm_nt(last, ref[...]) for ref in (q_ref, k_ref, v_ref)], 0).astype(BF16)
     n = lax.axis_size("ctx")
     me = lax.axis_index("ctx")
     right, left = lax.rem(me + 1, n), lax.rem(me + n - 1, n)
-    barrier = pltpu.get_barrier_semaphore()
-    for other in (right, left):
-        pl.semaphore_signal(barrier, inc=1, device_id={"ctx": other}, device_id_type=pl.DeviceIdType.MESH)
-    pl.semaphore_wait(barrier, 2)
-    send(tails, got, sems.at[0], sems.at[1], "ctx", right).wait()
-    halo_ref[...] = jnp.where(me > 0, got[...].astype(F32), 0.0).astype(BF16)
+    copy = pltpu.make_async_remote_copy(
+        src_ref=tails, dst_ref=got, send_sem=sems.at[0], recv_sem=sems.at[1],
+        device_id={"ctx": right}, device_id_type=pl.DeviceIdType.MESH)
+
+    @pl.when(pl.program_id(0) == 0)
+    def _():
+        barrier = pltpu.get_barrier_semaphore()
+        for other in (right, left):
+            pl.semaphore_signal(barrier, inc=1, device_id={"ctx": other}, device_id_type=pl.DeviceIdType.MESH)
+        shape = (8, rows)
+        last = (lax.broadcasted_iota(jnp.int32, shape, 0) + (rows - 8) == lax.broadcasted_iota(jnp.int32, shape, 1)).astype(BF16)
+        tails[...] = jnp.concatenate([mm_nt(last, ref[...]) for ref in (q_ref, k_ref, v_ref)], 0).astype(BF16)
+        pl.semaphore_wait(barrier, 2)
+        copy.start()
+
+    powers_kernel(dec_ref, res_ref, times_ref, pick_ref, hi_ref, lo_ref, eye_ref, pow_ref, spec_ref, flat_ref)
+
+    @pl.when(pl.program_id(0) == pl.num_programs(0) - 1)
+    def _():
+        copy.wait()
+        halo_ref[...] = jnp.where(me > 0, got[...].astype(F32), 0.0).astype(BF16)
 
 
 def gather_kernel(rows, state_ref, dec_ref, in_ref, out, got, send_sem, recv_sem):
@@ -271,8 +291,8 @@
     in_ref[modes:, :] = r
 
 
-def reduce_kernel(scale, part_ref, head_ref, total_ref, halo_ref, parted, got, mine, full, heads,
-                  send_sem, recv_sem, back_send, back_recv, halo_sem):
+def reduce_kernel(scale, taps, block, part_ref, head_ref, gq_ref, gk_ref, gv_ref, w_ref, place_ref, shift_ref, wide_ref,
+                  total_ref, oq_ref, ok_ref, ov_ref, parted, got, mine, full, heads, ends, send_sem, recv_sem, back_send, back_recv, halo_sem):
     n = lax.axis_size("ctx")
     width = parted.shape[2]
     for p in range(n):
@@ -282,6 +302,17 @@
     copies = []
     for d in range(1, n):
         copies.append(send(parted.at[where[d]], got.at[d], send_sem.at[d], recv_sem.at[d], "ctx", where[d]))
+    halo.wait()
+    ends[...] = jnp.where(me < n - 1, heads[...].astype(F32), 0.0).astype(BF16)
+    count = gq_ref.shape[0] // block
+
+    def step(b, carry):
+        at = pl.ds(pl.multiple_of(b * block, block), block)
+        oq_ref[at, :], ok_ref[at, :], ov_ref[at, :] = anti_taps(
+            taps, (gq_ref[at, :], gk_ref[at, :], gv_ref[at, :]), ends[:, at], w_ref[:, at], place_ref, shift_ref, wide_ref)
+        return carry
+
+    lax.fori_loop(0, count // 2, step, 0)
     total = parted[me].astype(F32)
     for d in range(1, n):
         copies[d - 1].wait()
@@ -291,8 +322,7 @@
     for d in range(1, n):
         copies.append(send(mine, full.at[d], back_send.at[d], back_recv.at[d], "ctx", where[d]))
     full[0] = mine[...]
-    halo.wait()
-    halo_ref[...] = jnp.where(me < n - 1, heads[...].astype(F32), 0.0).astype(BF16)
+    lax.fori_loop(count // 2, count, step, 0)
     for copy in copies:
         copy.wait()
     for p in range(n):
@@ -343,15 +373,6 @@
     params = pltpu.CompilerParams(vmem_limit_bytes=60 * 1024 * 1024)
     dma = pltpu.SemaphoreType.DMA
     vmem = pl.BlockSpec(memory_space=pltpu.VMEM)
-    left = pl.pallas_call(
-        halo_kernel,
-        in_specs=[vmem] * 3,
-        out_specs=vmem,
-        out_shape=shape(24, channels, kind=BF16),
-        scratch_shapes=[pltpu.VMEM((24, channels), BF16)] * 2 + [dma((2,))],
-        compiler_params=pltpu.CompilerParams(collective_id=2, has_side_effects=True, vmem_limit_bytes=60 * 1024 * 1024),
-        name="halo",
-    )(queries, key_signal, value_signal)
     w_flat = jnp.concatenate([short_weight.reshape(3 * taps, channels), jnp.zeros((24 - 3 * taps, channels), F32)], 0)
     skip = skip_gain[None, :]
     both = [np.zeros((2 * rows, taps * rows), np.float32) for _ in range(2)]
@@ -365,14 +386,15 @@
         spread_w[i, i * rows : (i + 1) * rows] = 1
     spread_w = jnp.asarray(np.tile(spread_w, (3, 1)), BF16)
 
-    args = (tab["times"], tab["pick"], tab["spec_hi"], tab["spec_lo"], jnp.eye(modes, dtype=BF16))
-    powers, spec, flats = pl.pallas_call(
-        powers_kernel,
+    args = (tab["times"], tab["pick"], tab["spec_hi"], tab["spec_lo"], jnp.eye(modes, dtype=BF16), queries, key_signal, value_signal)
+    powers, spec, flats, left = pl.pallas_call(
+        first_kernel,
         grid=grid,
         in_specs=[tall(modes), tall(modes)] + [whole(x) for x in args],
-        out_specs=[tall(wide), tall(2 * rows), flat(2 * modes)],
-        out_shape=[shape(channels, wide), shape(channels, 2 * rows), shape(2 * modes, channels)],
-        compiler_params=params,
+        out_specs=[tall(wide), tall(2 * rows), flat(2 * modes), pl.BlockSpec((24, channels), lambda i: (0, 0))],
+        out_shape=[shape(channels, wide), shape(channels, 2 * rows), shape(2 * modes, channels), shape(24, channels, kind=BF16)],
+        scratch_shapes=[pltpu.VMEM((24, channels), BF16)] * 2 + [dma((2,))],
+        compiler_params=pltpu.CompilerParams(collective_id=2, has_side_effects=True, vmem_limit_bytes=60 * 1024 * 1024),
         cost_estimate=pl.CostEstimate(flops=10**9, bytes_accessed=5 * 10**6, transcendentals=10**6),
         name="powers",
     )(decay_rates, residues, *args)
@@ -418,33 +440,33 @@
     width = channels // devices
     if width % 128 == 0:
         height = modes + 32
-        totals, right = pl.pallas_call(
-            functools.partial(reduce_kernel, scale),
-            in_specs=[vmem] * 2,
-            out_specs=[vmem] * 2,
-            out_shape=[shape(height, channels), shape(24, channels, kind=BF16)],
+        totals, *grads = pl.pallas_call(
+            functools.partial(reduce_kernel, scale, taps, block),
+            in_specs=[vmem] * 9,
+            out_specs=[vmem] * 4,
+            out_shape=[shape(height, channels)] + [shape(channels, rows, kind=BF16)] * 3,
             scratch_shapes=[
                 pltpu.VMEM((devices, height, width), BF16), pltpu.VMEM((devices, height, width), BF16),
                 pltpu.VMEM((height, width), BF16), pltpu.VMEM((devices, height, width), BF16),
-                pltpu.VMEM((24, channels), BF16),
+                pltpu.VMEM((24, channels), BF16), pltpu.VMEM((24, channels), BF16),
                 dma((devices,)), dma((devices,)), dma((devices,)), dma((devices,)), dma((2,)),
             ],
             compiler_params=pltpu.CompilerParams(collective_id=1, has_side_effects=True, vmem_limit_bytes=60 * 1024 * 1024),
             name="reduce",
-        )(part, heads)
+        )(part, heads, gq, gk, gv, w_flat, head, after, spread_w)
     else:
         right = passed_along(heads, "ctx", -1)
         totals = lax.psum(part, "ctx") * scale
-    grads = pl.pallas_call(
-        functools.partial(last_kernel, taps),
-        grid=grid,
-        in_specs=[tall(rows)] * 3 + [flat(24), flat(24), whole(head), whole(after), whole(spread_w)],
-        out_specs=[tall(rows)] * 3,
-        out_shape=[shape(channels, rows, kind=BF16)] * 3,
-        compiler_params=params,
-        cost_estimate=pl.CostEstimate(flops=10**9, bytes_accessed=5 * 10**6, transcendentals=0),
-        name="last",
-    )(gq, gk, gv, right, w_flat, head, after, spread_w)
+        grads = pl.pallas_call(
+            functools.partial(last_kernel, taps),
+            grid=grid,
+            in_specs=[tall(rows)] * 3 + [flat(24), flat(24), whole(head), whole(after), whole(spread_w)],
+            out_specs=[tall(rows)] * 3,
+            out_shape=[shape(channels, rows, kind=BF16)] * 3,
+            compiler_params=params,
+            cost_estimate=pl.CostEstimate(flops=10**9, bytes_accessed=5 * 10**6, transcendentals=0),
+            name="last",
+        )(gq, gk, gv, right, w_flat, head, after, spread_w)
     return (
         mixed,
         *grads,

time: 109 us -> 104 us (0.954)
  Pallas kernels: 101 us -> 87.4 us
  local copies, waits for them, and re-layouts: 6.82 us -> 14.8 us
    pallas_call x4 -> x2, Pallas kernels: 52 us -> 37.8 us  [the longest x1 21.6 us: per_device(): pl.pallas_call(functools.partial(reduce_kernel, scale, taps, block), in_s...]
    unnamed x8 -> x9, local copies, waits for them, and re-layouts: 2.67 us -> 7.93 us
where the time goes in v3:
time: 104 us; the launch traced here: 103 us
  Pallas kernels  87.4 us (84%)
  local copies, waits for them, and re-layouts  14.8 us (14%)
    pallas_call x1, Pallas kernels, per_device(): pl.pallas_call(functools.partial(reduce_kernel, scale, taps, block), in_s...  21.6 us
    pallas_call x1, Pallas kernels, per_device(): pl.pallas_call(functools.partial(near_kernel, taps), grid=grid, in_specs=...  18.2 us
    pallas_call x1, Pallas kernels, per_device(): pl.pallas_call(functools.partial(far_kernel, taps), grid=grid, in_specs=[...  17 us
    pallas_call x1, Pallas kernels, per_device(): pl.pallas_call(first_kernel, grid=grid, in_specs=[tall(modes), tall(modes...  16.3 us
    pallas_call x1, Pallas kernels, per_device(): pl.pallas_call(functools.partial(gather_kernel, rows), in_specs=[vmem] *...  14.3 us
    unnamed x9, local copies, waits for them, and re-layouts  7.93 us

profile of v3, /device:TPU:0, one launch (start us, length us, event | category | flops | bytes accessed | tf_op | source)
XLA Modules:
  0.0 103.5 jit_solution(5045532193697534021)
XLA Ops:
  0.6 0.6 fusion.eye_ref
  1.2 1.0 reshape.20
  2.2 0.7 concatenate.3.w_ref
  2.9 2.2 %copy.34.res_ref = f32[2048,16]{1,0:T(8,128)} copy(f32[2048,16]{0,1:T(8,128)} %param.31) | data formatting | bytes 262144 | tf_op args[5]
  5.1 2.2 %copy.33.dec_ref = f32[2048,16]{1,0:T(8,128)} copy(f32[2048,16]{0,1:T(8,128)} %param.32) | data formatting | bytes 262144 | tf_op args[6]
  7.3 16.3 %powers.1 = (f32[2048,256]{1,0:T(8,128)}, f32[2048,256]{1,0:T(8,128)}, f32[32,2048]{1,0:T(8,128)}, bf16[24,2048]{1,0:T(8,128)(2,1)}) custom-call(f32[2048,16]{1,0:T(8,128)} %copy.33.dec_ref, f32[2048,16]{1,0:T(8,128)} %copy.34.res_ref, bf16[16,256]{1,0:T(8,128)(2,1)} %constant.50.clone.times_ref, bf16[16,256]{1,0:T(8,128)(2,1)} %constant.51.clone.pick_ref, ...), custom_call_target="tpu_custom_call" | custom-call | flops 1000000000 | bytes 5000000 | tf_op jit(solution)/shard_map/powers/pallas_call | solution.py:390
  23.6 18.2 %near.1 = (bf16[2048,128]{1,0:T(8,128)(2,1)}, bf16[2048,128]{1,0:T(8,128)(2,1)}, bf16[2048,128]{1,0:T(8,128)(2,1)}, f32[2048,128]{1,0:T(8,128)}, f32[2048,128]{1...) custom-call(bf16[2048,128]{1,0:T(8,128)(2,1)} %q_ref.5, bf16[2048,128]{1,0:T(8,128)(2,1)} %k_ref.5, ...), custom_call_target="tpu_custom_call" | custom-call | tf_op jit(solution)/shard_map/near/pallas_call | solution.py:403
  41.8 14.3 %gather.1.all_ref = f32[32,2048]{1,0:T(8,128)} custom-call(f32[32,2048]{1,0:T(8,128)} %get-tuple-element.36.state_ref, f32[32,2048]{1,0:T(8,128)} %get-tuple-element.37.dec_ref.amp_ref), custom_call_target="tpu_custom_call" | custom-call | tf_op jit(solution)/shard_map/gather/pallas_call | solution.py:413
  56.1 0.5 broadcast_in_dim.8.ones_ref
  56.7 17.0 %far.1 = (bf16[2048,128]{1,0:T(8,128)(2,1)}, bf16[2048,128]{1,0:T(8,128)(2,1)}, bf16[2048,128]{1,0:T(8,128)(2,1)}, bf16[2048,128]{1,0:T(8,128)(2,1)}, bf16[24,2048]{1,0:T(8,128)(2,1)}, /*index=5*/f32[48,2048]{1,0:T(8,128)}) custom-call(bf16[2048,128]{1,0:T(8,128)(2,1)} %q_ref.5, bf16[2048,128]{1,0:T(8,128)(2,1)} %k_ref.5, bf16[2048,128]{1,0:T(8,128)(2,1)} %v_ref.5, ...), custom_call_target="tpu_custom_call" | custom-call | tf_op jit(solution)/shard_map/far/pallas_call | solution.py:426
  73.7 21.6 %reduce.1 = (f32[48,2048]{1,0:T(8,128)}, bf16[2048,128]{1,0:T(8,128)(2,1)}, bf16[2048,128]{1,0:T(8,128)(2,1)}, bf16[2048,128]{1,0:T(8,128)(2,1)}) custom-call(f32[48,2048]{1,0:T(8,128)} %get-tuple-element.40.part_ref, bf16[24,2048]{1,0:T(8,128)(2,1)} %get-tuple-element.41.head_ref, bf16[2048,128]{1,0:T(8,128)(2,1)} %get-tuple-element.42.gq_ref, ...), custom_call_target="tpu_custom_call" | custom-call | tf_op jit(solution)/shard_map/reduce/pallas_call | solution.py:443
  95.3 0.0 copy-start.1
  95.3 0.0 copy-start
  95.3 1.5 %slice.11 = f32[1,2048]{1,0:T(1,128)} slice(f32[48,2048]{1,0:T(8,128)} %get-tuple-element.48), slice={[37:38], [0:2048]} | slice | bytes 16384 | tf_op jit(solution)/shard_map/slice | solution.py:475
  96.8 1.6 %slice_bitcast_fusion = f32[2048,16]{0,1:T(8,128)} fusion(f32[48,2048]{1,0:T(8,128)} %get-tuple-element.48), kind=kLoop, calls=%fused_computation | loop fusion | bytes 262144 | tf_op jit(solution)/shard_map/transpose | solution.py:474
  98.4 0.9 slice.9
  99.3 0.7 reshape.21
  100.0 1.9 %copy.38 = bf16[2048,128]{1,0:T(8,128)(2,1)} copy(bf16[2048,128]{1,0:T(8,128)(2,1)} %get-tuple-element.57) | data formatting | bytes 1048576
  101.9 0.0 copy-done.1
  101.9 0.8 copy.39
  102.7 0.0 copy-done
  102.7 0.8 copy.40
Async XLA Ops:
  95.3 6.6 %copy-start.1 = (bf16[2048,128]{1,0:T(8,128)(2,1)S(1)}, bf16[2048,128]{1,0:T(8,128)(2,1)}, u32[]{:S(2)}) copy-start(bf16[2048,128]{1,0:T(8,128)(2,1)} %get-tuple-element.58) | copy-start | bytes 1572868
  95.3 7.4 %copy-start = (bf16[2048,128]{1,0:T(8,128)(2,1)S(1)}, bf16[2048,128]{1,0:T(8,128)(2,1)}, u32[]{:S(2)}) copy-start(bf16[2048,128]{1,0:T(8,128)(2,1)} %get-tuple-element.59) | copy-start | bytes 1572868
